TPU v7x, 512 devices: a whole 4x8x8 slice. The times are simulated.
512 devices in a mesh: occ: 64 (over x, y, core), aux: 8 (over z).
Axes of the slice: x: 4, y: 8, z: 8, core: 2. Of those that a mesh axis runs over, the one named last changes fastest.
Arguments:
- ao_blocks: bfloat16 [256, 256, 8192], P('occ', None, 'aux'), may hold values from -0.59765625 to 0.59765625
- pno_coef: bfloat16 [1024, 256, 200], P('occ'), may hold values from -0.375 to 0.375
- pno_energy: float32 [1024, 200], P('occ'), may hold values from 0.3 to 3
- occ_energy: float32 [256], replicated, may hold values from -1.5 to -0.3
- pair_partner: int32 [1024], P('occ'), may hold values from 0 to 255, as said below
- pno_count: int32 [1024], P('occ'), may hold values from 40 to 200, as said below
Outputs:
- amplitudes: float32 [1024, 200, 200], P(('occ', 'aux'))
- orbital_pair_energy: float32 [256], P('occ')
Inputs may be any that keep to these rules, and one draw needn't show every extreme that they name: pair_partner[s] differs from own(s) and is an orbital owned by the same index of occ as own(s), or by the index just below or just above it. `pno_count`: every count is a multiple of 8; in every block of 16 pairs one count is 200 and one is 40.
All inputs are finite; a program needn't handle non-finite values.
Results may differ from a plain program's by a relative error of at most 0.0041.
Values may be sent and summed in bfloat16 or wider, within the bound.
A program may use at most 128 MiB of HBM per device.

v0:
```python
import jax
import jax.numpy as jnp
from jax import lax
from jax.sharding import PartitionSpec as P


def padded(cells, sides, width):
    for axis, dim in sides:
        count = lax.axis_size(axis)
        ends = count - 1
        head = lax.slice_in_dim(cells, 0, width, axis=dim)
        tail = lax.slice_in_dim(cells, cells.shape[dim] - width, cells.shape[dim], axis=dim)
        cells = jnp.concatenate(
            [
                lax.ppermute(tail, axis, [(i, (i + 1) % count) for i in range(ends)]),
                cells,
                lax.ppermute(head, axis, [((i + 1) % count, i) for i in range(ends)]),
            ],
            axis=dim,
        )
    return cells


def shards(ao_blocks, pno_coef, pno_energy, occ_energy, pair_partner, pno_count):
    orb_dev = ao_blocks.shape[0]
    virtuals = ao_blocks.shape[1]
    aux_block = ao_blocks.shape[2]
    pair_dev = pno_coef.shape[0]
    pno_max = pno_coef.shape[2]
    per_orbital = pair_dev // orb_dev
    occ_place = lax.axis_index("occ")
    aux_place = lax.axis_index("aux")
    columns = jnp.arange(pno_max, dtype=jnp.int32)
    kept_mask = (columns[None, :] < pno_count[:, None]).astype(jnp.bfloat16)
    masked_coef = pno_coef * kept_mask[:, None, :]
    projected_own = (
        jnp.einsum(
            "ornp,onk->orpk",
            masked_coef.reshape(orb_dev, per_orbital, virtuals, pno_max),
            ao_blocks,
            preferred_element_type=jnp.float32,
        )
        .astype(jnp.bfloat16)
        .reshape(pair_dev, pno_max, aux_block)
    )
    nearby = padded(ao_blocks, (("occ", 0),), orb_dev)
    window_slot = pair_partner - (occ_place - 1) * orb_dev
    partner_blocks = jnp.take(nearby, window_slot, axis=0)
    projected_partner = jnp.einsum(
        "snp,snk->spk", masked_coef, partner_blocks, preferred_element_type=jnp.float32
    ).astype(jnp.bfloat16)
    partials = jnp.einsum(
        "spk,sqk->spq", projected_own, projected_partner, preferred_element_type=jnp.float32
    )
    share_rows = pair_dev // lax.axis_size("aux")
    first_row = aux_place * share_rows
    totals = lax.psum(partials, "aux")
    exchange_ints = lax.dynamic_slice_in_dim(totals, first_row, share_rows, 0)
    own_orbital = occ_place * orb_dev + jnp.arange(pair_dev, dtype=jnp.int32) // per_orbital
    mine_owner = lax.dynamic_slice_in_dim(own_orbital, first_row, share_rows, 0)
    mine_partner = lax.dynamic_slice_in_dim(pair_partner, first_row, share_rows, 0)
    energies = lax.dynamic_slice_in_dim(pno_energy, first_row, share_rows, 0)
    shift_occ = occ_energy[mine_owner] + occ_energy[mine_partner]
    denominator = energies[:, :, None] + energies[:, None, :] - shift_occ[:, None, None]
    amplitudes = -exchange_ints / denominator
    pair_energy = jnp.sum(
        (2.0 * exchange_ints - jnp.swapaxes(exchange_ints, 1, 2)) * amplitudes, axis=(1, 2)
    )
    half_energy = 0.5 * pair_energy
    orbital_ids = jnp.arange(occ_energy.shape[0], dtype=jnp.int32)
    hits = (orbital_ids[None, :] == mine_owner[:, None]).astype(jnp.float32) + (
        orbital_ids[None, :] == mine_partner[:, None]
    ).astype(jnp.float32)
    spread = jnp.sum(hits * half_energy[:, None], axis=0)
    whole_sum = lax.psum(spread, ("occ", "aux"))
    orbital = lax.dynamic_slice_in_dim(whole_sum, occ_place * orb_dev, orb_dev, 0)
    return (amplitudes, orbital)


def solution(mesh):
    return jax.shard_map(
        shards,
        mesh=mesh,
        in_specs=(
            P("occ", None, "aux"),
            P("occ", None, None),
            P("occ", None),
            P(),
            P("occ"),
            P("occ"),
        ),
        out_specs=(P(("occ", "aux"), None, None), P("occ")),
        check_vma=False,
    )
```

profile of v0, /device:TPU:1, one launch (start us, length us, event | category | flops | bytes accessed | tf_op | source)
XLA Modules:
  0.0 275.3 jit_solution(15171100014383080903)
XLA Ops:
  7.2 0.0 copy-start
  7.2 0.0 copy-start.2
  7.2 0.0 all-reduce.2.cloned.1.call-start
  7.2 4.7 %collective-permute-start = (bf16[4,256,1024]{2,1,0:T(8,128)(2,1)}, bf16[4,256,1024]{2,1,0:T(8,128)(2,1)}, u32[]{:S(2)}, u32[]{:S(2)}) collective-permute-start(bf16[4,256,1024]{2,1,0:T(8,128)(2,1)} %param.6), channel_id=1, source_target_pairs={{0,8},{8,16},{16,24},{24,32},{32,40},{40,48},{48,56},{56,64},{64,7... | collective-permute-start | bytes 6291464 | tf_op jit(solution)/shard_map/ppermute | solution.py:15
  12.0 6.8 %collective-permute-start.1 = (bf16[4,256,1024]{2,1,0:T(8,128)(2,1)}, bf16[4,256,1024]{2,1,0:T(8,128)(2,1)}, u32[]{:S(2)}, u32[]{:S(2)}) collective-permute-start(bf16[4,256,1024]{2,1,0:T(8,128)(2,1)} %param.6), channel_id=1, source_target_pairs={{8,0},{16,8},{24,16},{32,24},{40,32},{48,40},{56,48},{64,56},{72,6... | collective-permute-start | bytes 6291464 | tf_op jit(solution)/shard_map/ppermute | solution.py:17
  18.7 0.7 compare_and_fusion
  19.4 0.7 fusion.13
  20.1 1.9 broadcast_multiply_fusion
  22.0 0.0 copy-start.3
  22.1 0.0 copy-done.2
  22.1 4.7 %convolution_convert_fusion = bf16[4,4,200,1024]{3,2,1,0:T(8,128)(2,1)} fusion(bf16[4,4,256,200]{2,3,1,0:T(8,128)(2,1)S(1)} %bitcast.16, bf16[4,256,1024]{2,1,0:T(8,128)(2,1)S(1)} %copy-done.2), kind=kOutput, calls=%fused_computation.8 | convolution fusion | flops 1680998400 | bytes 10289152 | tf_op jit(solution)/shard_map/ornp,onk->orpk/dot_general | solution.py:37
  26.8 0.0 copy-done.3
  26.8 8.5 %collective-permute-done = bf16[4,256,1024]{2,1,0:T(8,128)(2,1)} collective-permute-done((bf16[4,256,1024]{2,1,0:T(8,128)(2,1)}, bf16[4,256,1024]{2,1,0:T(8,128)(2,1)}, u32[]{:S(2)}, u32[]{:S(2)}) %collective-permute-start) | collective-permute-done | bytes 2097184 | tf_op jit(solution)/shard_map/ppermute | solution.py:15
  35.2 4.4 %collective-permute-done.1 = bf16[4,256,1024]{2,1,0:T(8,128)(2,1)} collective-permute-done((bf16[4,256,1024]{2,1,0:T(8,128)(2,1)}, bf16[4,256,1024]{2,1,0:T(8,128)(2,1)}, u32[]{:S(2)}, u32[]{:S(2)}) %collective-permute-start.1) | collective-permute-done | bytes 2097184 | tf_op jit(solution)/shard_map/ppermute | solution.py:17
  39.6 5.5 %pad_maximum_fusion = bf16[12,256,1024]{2,1,0:T(8,128)(2,1)} fusion(bf16[4,256,1024]{2,1,0:T(8,128)(2,1)} %collective-permute-done.1, bf16[4,256,1024]{2,1,0:T(8,128)(2,1)S(1)} %copy-done.2, bf16[4,256,1024]{2,1,0:T(8,128)(2,1)} %collective-permute-done), kind=kLoop, calls=%fused_computation.7 | loop fusion | flops 6291456 | bytes 12582912 | tf_op jit(solution)/shard_map/concatenate | solution.py:13
  45.1 7.6 %gather_fusion = bf16[16,256,1024]{2,1,0:T(8,128)(2,1)} fusion(bf16[12,256,1024]{2,1,0:T(8,128)(2,1)} %pad_maximum_fusion, s32[1024]{0:T(1024)S(1)} %pad_clamp_fusion.2), kind=kCustom, calls=%fused_computation | custom fusion | bytes 16777280 | tf_op jit(solution)/shard_map/jit(_take)/gather | solution.py:48
  52.7 0.0 copy-done.4
  52.7 10.8 %fusion.9 = f32[16,200,200]{2,1,0:T(8,128)} fusion(bf16[16,200,1024]{2,1,0:T(8,128)(2,1)} %bitcast.17, bf16[16,256,200]{1,2,0:T(8,128)(2,1)S(1)} %copy-done.4, bf16[16,256,1024]{2,1,0:T(8,128)(2,1)} %gather_fusion, pred[16]{0:T(512)(128)(4,1)S(1)} %get-tuple-element.12), kind=kOutput, calls=%fused_computation.11 | convolution fusion | flops 2995912704 | bytes 19140624 | tf_op jit(solution)/shard_map/spk,sqk->spq/dot_general | solution.py:52
  63.5 0.0 all-reduce.2.cloned.1.call-update
  63.5 0.0 copy-done.5
  63.5 0.1 compare_select_fusion
  63.6 0.6 gather_fusion.1
  64.3 0.6 gather_fusion.2
  64.9 0.0 copy-done
  64.9 102.3 %all-reduce.2.cloned.1.call-done = f32[16,200,200]{2,1,0:T(8,128)} async-done(((f32[16,200,200]{2,1,0:T(8,128)}), f32[16,200,200]{2,1,0:T(8,128)}) %all-reduce.2.cloned.1.call-update) | async-done | bytes 2560016 | tf_op jit(solution)/shard_map/psum | solution.py:57
  167.2 1.0 constant_dynamic-slice_fusion.1
  168.2 0.2 copy.14
  168.4 1.3 fusion.12
  169.8 0.9 copy.16
  170.7 0.1 fusion.16
  170.8 97.1 %psum.15 = f32[256]{0:T(256)S(1)} all-reduce(f32[256]{0:T(256)S(1)} %fusion.16), channel_id=1, replica_groups=mesh['occ'=64,'aux'=8] {'occ','aux'}, use_global_device_ids=true, to_apply=%region_3.4 | all-reduce | flops 256 | bytes 2048 | tf_op jit(solution)/shard_map/psum | solution.py:75
  267.9 0.6 dynamic_slice.19
  (11 shorter events, 0.0 us)
Async XLA Ops:
  7.2 57.8 %copy-start = (f32[16,200]{1,0:T(8,128)S(1)}, f32[16,200]{1,0:T(8,128)}, u32[]{:S(2)}) copy-start(f32[16,200]{1,0:T(8,128)} %param.8) | copy-start | bytes 38404
  7.2 14.9 %copy-start.2 = (bf16[4,256,1024]{2,1,0:T(8,128)(2,1)S(1)}, bf16[4,256,1024]{2,1,0:T(8,128)(2,1)}, u32[]{:S(2)}) copy-start(bf16[4,256,1024]{2,1,0:T(8,128)(2,1)} %param.6) | copy-start | bytes 6291460
  7.2 160.0 %all-reduce.2.cloned.1.call-start = ((), (), s32[]{:S(2)}) async-start(), calls=%async_computation | async-start | bytes 6553600 | tf_op jit(solution)/shard_map/psum | solution.py:57
  7.2 28.0 %collective-permute-start = (bf16[4,256,1024]{2,1,0:T(8,128)(2,1)}, bf16[4,256,1024]{2,1,0:T(8,128)(2,1)}, u32[]{:S(2)}, u32[]{:S(2)}) collective-permute-start(bf16[4,256,1024]{2,1,0:T(8,128)(2,1)} %param.6), channel_id=1, source_target_pairs={{0,8},{8,16},{16,24},{24,32},{32,40},{40,48},{48,56},{56,64},{64,7... | collective-permute-start | bytes 6291464 | tf_op jit(solution)/shard_map/ppermute | solution.py:15
  12.0 27.7 %collective-permute-start.1 = (bf16[4,256,1024]{2,1,0:T(8,128)(2,1)}, bf16[4,256,1024]{2,1,0:T(8,128)(2,1)}, u32[]{:S(2)}, u32[]{:S(2)}) collective-permute-start(bf16[4,256,1024]{2,1,0:T(8,128)(2,1)} %param.6), channel_id=1, source_target_pairs={{8,0},{16,8},{24,16},{32,24},{40,32},{48,40},{56,48},{64,56},{72,6... | collective-permute-start | bytes 6291464 | tf_op jit(solution)/shard_map/ppermute | solution.py:17
  22.0 4.7 %copy-start.3 = (bf16[16,256,200]{1,2,0:T(8,128)(2,1)}, bf16[16,256,200]{1,2,0:T(8,128)(2,1)S(1)}, u32[]{:S(2)}) copy-start(bf16[16,256,200]{1,2,0:T(8,128)(2,1)S(1)} %broadcast_multiply_fusion) | copy-start | bytes 4915204
  45.1 7.6 %copy-start.4 = (bf16[16,256,200]{1,2,0:T(8,128)(2,1)S(1)}, bf16[16,256,200]{1,2,0:T(8,128)(2,1)}, u32[]{:S(2)}) copy-start(bf16[16,256,200]{1,2,0:T(8,128)(2,1)} %copy-done.3) | copy-start | bytes 4915204
  52.7 10.8 %copy-start.5 = (s32[16]{0:T(128)S(1)}, s32[16]{0:T(128)}, u32[]{:S(2)}) copy-start(s32[16]{0:T(128)} %param.10) | copy-start | bytes 196
  52.7 10.9 %copy-start.1 = (f32[256]{0:T(256)S(1)}, f32[256]{0:T(256)}, u32[]{:S(2)}) copy-start(f32[256]{0:T(256)} %param.9) | copy-start | bytes 3076
Sparse Core Ops, SparseCore 0:
  63.6 103.5 all-reduce.1
where the time goes:
time: 276 us; the launch traced here: 275 us
  waiting for transfers between devices  115 us (42%)
  blocking collectives  97.1 us (35%)
  matrix products  15.4 us (6%)
  between operations  14.1 us (5%)
  local copies, waits for them, and re-layouts  11.6 us (4%)
  starting transfers between devices  11.5 us (4%)
  other arithmetic  10.3 us (4%)
    psum x1, waiting for transfers between devices, shards(): totals = lax.psum(partials, 'aux')  102 us
    psum x1, blocking collectives, shards(): whole_sum = lax.psum(spread, ('occ', 'aux'))  97.1 us
    dot_general x1, matrix products, shards(): jnp.einsum('spk,sqk->spq', projected_own, projected_partner, preferred_el...  10.8 us
    ppermute x1, waiting for transfers between devices, padded(): lax.ppermute(tail, axis, [(i, (i + 1) % count) for i in range(ends)])  8.47 us
    gather x1, local copies, waits for them, and re-layouts, shards(): partner_blocks = jnp.take(nearby, window_slot, axis=0)  7.6 us
    ppermute x1, starting transfers between devices, padded(): lax.ppermute(head, axis, [((i + 1) % count, i) for i in range(ends)])  6.75 us
  transfers between devices with their start and end apart: 3, of which 3 were waited for; matrix products, arithmetic and copies ran while one was open for 3% of the time, Pallas kernels for 0%

commit v1 on v0

v1 whole, which is shorter than its diff:
```python
import functools

import jax
import jax.numpy as jnp
from jax import lax
from jax.experimental import pallas as pl
from jax.experimental.pallas import tpu as pltpu
from jax.sharding import PartitionSpec as P

MESH = pl.DeviceIdType.MESH
CHUNKS = 4
LANES = 128
F32 = jnp.float32
BF16 = jnp.bfloat16

ORDER = (
    (4, 0), (4, 1), (3, 1), (-3, 0),
    (3, 0), (-3, 1), (2, 0), (-2, 1),
    (2, 1), (-2, 0), (1, 0), (-1, 1),
    (1, 1), (-1, 0), (0, 0), (0, 1),
)
CHAINS = (
    (1, (0, 4, 6, 10)),
    (-1, (1, 5, 7, 11)),
    (1, (2, 8, 12)),
    (-1, (3, 9, 13)),
)
MESSAGES = 14


def nt_dot(left, right):
    return lax.dot_general(
        left, right, (((1,), (1,)), ((), ())), preferred_element_type=F32
    )


def kernel(
    occ_size, aux_size, partner, counts, occ_energy, energies, ao, coef,
    amp_out, orb_out,
    win0, win1, win2, win3, coefs, coef_t, own_proj, sums, parcel, landed,
    amp, gift, gifts, level, levels,
    local_sem, ao_send, ao_recv, chain_send, chain_recv, amp_sem,
    gift_send, gift_recv, level_send, level_recv,
):
    windows = (win0, win1, win2, win3)
    occ_me, aux_me = lax.axis_index("occ"), lax.axis_index("aux")
    right = lax.rem(occ_me + 1, occ_size)
    left = lax.rem(occ_me + occ_size - 1, occ_size)
    orbs = ao.shape[0]
    virtuals = ao.shape[1]
    width = ao.shape[2] // CHUNKS
    pairs, _, pnos = coef.shape
    per_orbital = pairs // orbs
    rows = own_proj.shape[1]

    def aux_at(distance):
        return lax.rem(aux_me + distance + aux_size, aux_size)

    barrier = pltpu.get_barrier_semaphore()
    for place in ((left, aux_me), (right, aux_me), (occ_me, aux_at(1)), (occ_me, aux_at(-1))):
        pl.semaphore_signal(barrier, inc=1, device_id=place, device_id_type=MESH)

    fetch_coef = pltpu.make_async_copy(coef, coefs, local_sem.at[CHUNKS])
    fetch_coef.start()
    fetches = []
    for k in range(CHUNKS):
        fetch = pltpu.make_async_copy(
            ao.at[:, :, pl.ds(k * width, width)],
            windows[k].at[pl.ds(orbs, orbs)],
            local_sem.at[k],
        )
        fetch.start()
        fetches.append(fetch)

    pl.semaphore_wait(barrier, 4)

    moves = []
    for k in range(CHUNKS):
        for side, (target, slot) in enumerate(((right, 0), (left, 2 * orbs))):
            move = pltpu.make_async_remote_copy(
                src_ref=ao.at[:, :, pl.ds(k * width, width)],
                dst_ref=windows[k].at[pl.ds(slot, orbs)],
                send_sem=ao_send.at[side, k],
                recv_sem=ao_recv.at[side, k],
                device_id=(target, aux_me),
                device_id_type=MESH,
            )
            move.start()
            moves.append(move)

    fetch_coef.wait()
    lanes = lax.broadcasted_iota(jnp.int32, (virtuals, pnos), 1)

    def turn(s, carry):
        kept = (lanes < counts[s]).astype(F32)
        flipped = (coefs[s].astype(F32) * kept).T
        coef_t[s] = jnp.zeros(coef_t.shape[1:], BF16)
        coef_t[s, :pnos] = flipped.astype(BF16)
        return carry

    lax.fori_loop(0, pairs, turn, 0)

    for k in range(CHUNKS):
        fetches[k].wait()

        def project(s, carry):
            block = windows[k][orbs + s // per_orbital]
            own = jnp.dot(coef_t[s, :rows], block, preferred_element_type=F32)
            own_proj[s, :, k * width:(k + 1) * width] = own.astype(BF16)
            return carry

        lax.fori_loop(0, pairs, project, 0, unroll=2)

    first_slot = (occ_me - 1) * orbs

    def slot_of(s):
        return jnp.clip(partner[s] - first_slot, 0, 3 * orbs - 1)

    def partial(s, k):
        block = windows[k][slot_of(s)]
        other = jnp.dot(coef_t[s], block, preferred_element_type=F32).astype(BF16)
        return nt_dot(own_proj[s, :, k * width:(k + 1) * width], other)

    for k in range(CHUNKS):
        moves[2 * k].wait_recv()
        moves[2 * k + 1].wait_recv()

        def accumulate(s, carry):
            if k == 0:
                sums[s] = partial(s, k)
            else:
                sums[s] = sums[s] + partial(s, k)
            return carry

        lax.fori_loop(0, pairs, accumulate, 0, unroll=2)

    def pair_at(position):
        distance, place = ORDER[position]
        return 2 * aux_at(distance) + place

    messages = {}

    def forward(chain, step):
        direction, positions = CHAINS[chain]
        number = sum(len(CHAINS[c][1]) for c in range(chain)) + step
        total = sums[pair_at(positions[step])]
        if step > 0:
            messages[chain, step - 1].wait_recv()
            total = total + landed[number - 1].astype(F32)
        parcel[number] = total.astype(BF16)
        message = pltpu.make_async_remote_copy(
            src_ref=parcel.at[number],
            dst_ref=landed.at[number],
            send_sem=chain_send.at[number],
            recv_sem=chain_recv.at[number],
            device_id=(occ_me, aux_at(direction)),
            device_id_type=MESH,
        )
        message.start()
        messages[chain, step] = message

    for step in range(4):
        for chain in range(4):
            if step < len(CHAINS[chain][1]):
                forward(chain, step)

    def closed(chain):
        steps = len(CHAINS[chain][1])
        number = sum(len(CHAINS[c][1]) for c in range(chain)) + steps - 1
        messages[chain, steps - 1].wait_recv()
        return landed[number].astype(F32)

    lane = lax.broadcasted_iota(jnp.int32, gift.shape, 1)
    spread = jnp.zeros(gift.shape, F32)
    writes = []
    for place, (long_chain, short_chain) in enumerate(((0, 3), (1, 2))):
        s = 2 * aux_me + place
        short = closed(short_chain)
        total = (sums[s] + short + closed(long_chain))[:pnos, :pnos]
        slot = slot_of(s)
        own_slot = orbs + s // per_orbital
        shift = occ_energy[first_slot + own_slot] + occ_energy[partner[s]]
        row = jnp.broadcast_to(energies[pl.ds(s, 1), :], (pnos, pnos))
        denominator = row + row.T - shift
        amplitude = -total / denominator
        amp[place] = amplitude
        write = pltpu.make_async_copy(amp.at[place], amp_out.at[place], amp_sem.at[place])
        write.start()
        writes.append(write)
        energy = jnp.sum((2.0 * total - total.T) * amplitude, axis=0, keepdims=True)
        energy = 0.5 * jnp.sum(energy, axis=1, keepdims=True)
        hits = (lane == own_slot).astype(F32) + (lane == slot).astype(F32)
        spread = spread + hits * energy

    gift[...] = spread
    passes = []
    for side, target in enumerate((right, left)):
        passed = pltpu.make_async_remote_copy(
            src_ref=gift,
            dst_ref=gifts.at[side],
            send_sem=gift_send.at[side],
            recv_sem=gift_recv.at[side],
            device_id=(target, aux_me),
            device_id_type=MESH,
        )
        passed.start()
        passes.append(passed)
    for passed in passes:
        passed.wait_recv()
    mine = (
        pltpu.roll(gifts[0], LANES - 2 * orbs, 1)
        + pltpu.roll(spread, LANES - orbs, 1)
        + gifts[1]
    )
    level[...] = mine
    levels[aux_me] = mine
    for distance in range(1, aux_size):
        passed = pltpu.make_async_remote_copy(
            src_ref=level,
            dst_ref=levels.at[aux_me],
            send_sem=level_send.at[distance],
            recv_sem=level_recv.at[distance],
            device_id=(occ_me, aux_at(distance)),
            device_id_type=MESH,
        )
        passed.start()
        passes.append(passed)
    for passed in passes[2:]:
        passed.wait_recv()
    whole = levels[0]
    for place in range(1, aux_size):
        whole = whole + levels[place]
    orb_out[...] = whole

    for move in moves:
        move.wait_send()
    for message in messages.values():
        message.wait_send()
    for passed in passes:
        passed.wait_send()
    for write in writes:
        write.wait()


def shards(mesh, ao_blocks, pno_coef, pno_energy, occ_energy, pair_partner, pno_count):
    orbs, virtuals, aux_block = ao_blocks.shape
    pairs, _, pnos = pno_coef.shape
    width = aux_block // CHUNKS
    occ_size, aux_size = mesh.shape["occ"], mesh.shape["aux"]
    rows = -(-pnos // 16) * 16
    padded = -(-pnos // LANES) * LANES
    share = pairs // aux_size
    smem = pl.BlockSpec(memory_space=pltpu.SMEM)
    vmem = pl.BlockSpec(memory_space=pltpu.VMEM)
    anywhere = pl.BlockSpec(memory_space=pl.ANY)
    dma = pltpu.SemaphoreType.DMA
    amplitudes, orbital = pl.pallas_call(
        functools.partial(kernel, occ_size, aux_size),
        out_shape=(
            jax.ShapeDtypeStruct((share, pnos, pnos), F32),
            jax.ShapeDtypeStruct((8, LANES), F32),
        ),
        in_specs=[smem, smem, smem, vmem, anywhere, anywhere],
        out_specs=(anywhere, vmem),
        scratch_shapes=[pltpu.VMEM((3 * orbs, virtuals, width), BF16)] * CHUNKS
        + [
            pltpu.VMEM((pairs, virtuals, pnos), BF16),
            pltpu.VMEM((pairs, padded, virtuals), BF16),
            pltpu.VMEM((pairs, rows, aux_block), BF16),
            pltpu.VMEM((pairs, rows, padded), F32),
            pltpu.VMEM((MESSAGES, rows, padded), BF16),
            pltpu.VMEM((MESSAGES, rows, padded), BF16),
            pltpu.VMEM((share, pnos, pnos), F32),
            pltpu.VMEM((8, LANES), F32),
            pltpu.VMEM((2, 8, LANES), F32),
            pltpu.VMEM((8, LANES), F32),
            pltpu.VMEM((aux_size, 8, LANES), F32),
            dma((CHUNKS + 1,)),
            dma((2, CHUNKS)),
            dma((2, CHUNKS)),
            dma((MESSAGES,)),
            dma((MESSAGES,)),
            dma((share,)),
            dma((2,)),
            dma((2,)),
            dma((aux_size,)),
            dma((aux_size,)),
        ],
        compiler_params=pltpu.CompilerParams(
            collective_id=0, has_side_effects=True, vmem_limit_bytes=60 * 1024 * 1024
        ),
    )(pair_partner, pno_count, occ_energy, pno_energy, ao_blocks, pno_coef)
    return amplitudes, orbital[0, :orbs]


def solution(mesh):
    return jax.shard_map(
        functools.partial(shards, mesh),
        mesh=mesh,
        in_specs=(
            P("occ", None, "aux"),
            P("occ", None, None),
            P("occ", None),
            P(),
            P("occ"),
            P("occ"),
        ),
        out_specs=(P(("occ", "aux"), None, None), P("occ")),
        check_vma=False,
    )
```

time: 276 us -> 76.1 us (0.28)
  waiting for transfers between devices: 115 us -> 0 us
  blocking collectives: 97.1 us -> 0 us
  Pallas kernels: 0 us -> 68.2 us
  matrix products: 15.4 us -> 0 us
  between operations: 14.1 us -> 0.64 us
  starting transfers between devices: 11.5 us -> 0 us
  other arithmetic: 10.3 us -> 0 us
  local copies, waits for them, and re-layouts: 11.6 us -> 6.69 us
    psum x1 -> x0, waiting for transfers between devices: 102 us -> none  [shards(): totals = lax.psum(partials, 'aux')]
    psum x1 -> x0, blocking collectives: 97.1 us -> none  [shards(): whole_sum = lax.psum(spread, ('occ', 'aux'))]
    pallas_call x0 -> x1, Pallas kernels: none -> 68.2 us  [shards(): pl.pallas_call(functools.partial(kernel, occ_size, aux_size), out_shape=(...]
    dot_general x2 -> x0, matrix products: 15.4 us -> none  [the longest x1 10.8 us: shards(): jnp.einsum('spk,sqk->spq', projected_own, projected_partner, preferred_el...]
    ppermute x2 -> x0, waiting for transfers between devices: 12.9 us -> none  [the longest x1 8.47 us: padded(): lax.ppermute(tail, axis, [(i, (i + 1) % count) for i in range(ends)])]
    ppermute x2 -> x0, starting transfers between devices: 11.5 us -> none  [the longest x1 6.75 us: padded(): lax.ppermute(head, axis, [((i + 1) % count, i) for i in range(ends)])]
    gather x3 -> x0, local copies, waits for them, and re-layouts: 8.88 us -> none  [the longest x1 7.6 us: shards(): partner_blocks = jnp.take(nearby, window_slot, axis=0)]
    concatenate x1 -> x0, other arithmetic: 5.48 us -> none  [padded(): jnp.concatenate([lax.ppermute(tail, axis, [(i, (i + 1) % count) for i in...]
  transfers between devices with their start and end apart: 3 -> 0, of which waited for: 3 -> 0; matrix products, arithmetic and copies ran while one was open for 3% -> 0% of each run, Pallas kernels for 0% -> 0%
where the time goes in v1:
time: 76.1 us; the launch traced here: 75.5 us
  Pallas kernels  68.2 us (90%)
  local copies, waits for them, and re-layouts  6.69 us (9%)
    pallas_call x1, Pallas kernels, shards(): pl.pallas_call(functools.partial(kernel, occ_size, aux_size), out_shape=(...  68.2 us
    unnamed x2, local copies, waits for them, and re-layouts  5.51 us

profile of v1, /device:TPU:1, one launch (start us, length us, event | category | flops | bytes accessed | tf_op | source)
XLA Modules:
  0.0 75.5 jit_solution(1457944329631439423)
XLA Ops:
  0.6 3.7 %copy.8.coef = bf16[16,256,200]{2,1,0:T(8,128)(2,1)} copy(bf16[16,256,200]{1,2,0:T(8,128)(2,1)} %param.7) | data formatting | bytes 3276800 | tf_op args[1]
  4.4 68.2 %shard_map.77 = (f32[2,200,200]{2,1,0:T(8,128)}, f32[8,128]{1,0:T(8,128)}) custom-call(s32[16]{0:T(128)} %partner.1, s32[16]{0:T(128)} %counts.1, f32[256]{0:T(256)} %occ_energy.1, f32[16,200]{1,0:T(8,128)} %energies.1, bf16[4,256,1024]{2,1,0:T(8,128)(2,1)} %ao.1, bf16[16,256,200]{2,1,0:T(8,128)(2,1)} %copy.8.coef), custom_call_target="tpu_custom_call" | custom-call | tf_op jit(solution)/shard_map/pallas_call | solution.py:257
  72.6 1.2 %slice_bitcast_fusion = f32[4]{0:T(128)} fusion(f32[8,128]{1,0:T(8,128)} %get-tuple-element.5), kind=kLoop, calls=%fused_computation | loop fusion | bytes 32 | tf_op jit(solution)/shard_map/squeeze | solution.py:293
  73.7 1.8 %copy.10 = f32[2,200,200]{2,1,0:T(8,128)} copy(f32[2,200,200]{2,1,0:T(8,128)} %get-tuple-element.8) | data formatting | bytes 640000

commit v2 on v1

--- a/solution.py
+++ b/solution.py
@@ -49,7 +49,7 @@
     orbs = ao.shape[0]
     virtuals = ao.shape[1]
     width = ao.shape[2] // CHUNKS
-    pairs, _, pnos = coef.shape
+    pairs, pnos, _ = coef.shape
     per_orbital = pairs // orbs
     rows = own_proj.shape[1]
 
@@ -89,16 +89,17 @@
             moves.append(move)
 
     fetch_coef.wait()
-    lanes = lax.broadcasted_iota(jnp.int32, (virtuals, pnos), 1)
-
-    def turn(s, carry):
-        kept = (lanes < counts[s]).astype(F32)
-        flipped = (coefs[s].astype(F32) * kept).T
-        coef_t[s] = jnp.zeros(coef_t.shape[1:], BF16)
-        coef_t[s, :pnos] = flipped.astype(BF16)
+    padded = coef_t.shape[1]
+    whole_rows = pnos // 16 * 16
+    places = lax.broadcasted_iota(jnp.int32, (pnos, virtuals), 0)
+
+    def mask(s, carry):
+        kept = jnp.where(places < counts[s], coefs[s].astype(F32), 0.0)
+        coef_t[s, whole_rows:] = jnp.zeros((padded - whole_rows, virtuals), BF16)
+        coef_t[s, :pnos] = kept.astype(BF16)
         return carry
 
-    lax.fori_loop(0, pairs, turn, 0)
+    lax.fori_loop(0, pairs, mask, 0)
 
     for k in range(CHUNKS):
         fetches[k].wait()
@@ -264,7 +265,7 @@
         out_specs=(anywhere, vmem),
         scratch_shapes=[pltpu.VMEM((3 * orbs, virtuals, width), BF16)] * CHUNKS
         + [
-            pltpu.VMEM((pairs, virtuals, pnos), BF16),
+            pltpu.VMEM((pairs, pnos, virtuals), BF16),
             pltpu.VMEM((pairs, padded, virtuals), BF16),
             pltpu.VMEM((pairs, rows, aux_block), BF16),
             pltpu.VMEM((pairs, rows, padded), F32),
@@ -289,7 +290,10 @@
         compiler_params=pltpu.CompilerParams(
             collective_id=0, has_side_effects=True, vmem_limit_bytes=60 * 1024 * 1024
         ),
-    )(pair_partner, pno_count, occ_energy, pno_energy, ao_blocks, pno_coef)
+    )(
+        pair_partner, pno_count, occ_energy, pno_energy, ao_blocks,
+        jnp.swapaxes(pno_coef, 1, 2),
+    )
     return amplitudes, orbital[0, :orbs]
 
 

time: 76.1 us -> 72.3 us (0.950)
  local copies, waits for them, and re-layouts: 6.69 us -> 2.97 us
    unnamed x2 -> x1, local copies, waits for them, and re-layouts: 5.51 us -> 1.78 us
where the time goes in v2:
time: 72.3 us; the launch traced here: 71.8 us
  Pallas kernels  68.2 us (94%)
  local copies, waits for them, and re-layouts  2.97 us (4%)
    pallas_call x1, Pallas kernels, shards(): pl.pallas_call(functools.partial(kernel, occ_size, aux_size), out_shape=(...  68.2 us
    unnamed x1, local copies, waits for them, and re-layouts  1.78 us

profile of v2, /device:TPU:1, one launch (start us, length us, event | category | flops | bytes accessed | tf_op | source)
XLA Modules:
  0.0 71.8 jit_solution(11199418553518467820)
XLA Ops:
  0.6 68.2 %shard_map.77 = (f32[2,200,200]{2,1,0:T(8,128)}, f32[8,128]{1,0:T(8,128)}) custom-call(s32[16]{0:T(128)} %partner.1, s32[16]{0:T(128)} %counts.1, f32[256]{0:T(256)} %occ_energy.1, f32[16,200]{1,0:T(8,128)} %energies.1, bf16[4,256,1024]{2,1,0:T(8,128)(2,1)} %ao.1, bf16[16,200,256]{2,1,0:T(8,128)(2,1)} %bitcast.3), custom_call_target="tpu_custom_call" | custom-call | tf_op jit(solution)/shard_map/pallas_call | solution.py:258
  68.8 1.2 %slice_bitcast_fusion = f32[4]{0:T(128)} fusion(f32[8,128]{1,0:T(8,128)} %get-tuple-element.5), kind=kLoop, calls=%fused_computation | loop fusion | bytes 32 | tf_op jit(solution)/shard_map/squeeze | solution.py:297
  70.0 1.8 %copy.9 = f32[2,200,200]{2,1,0:T(8,128)} copy(f32[2,200,200]{2,1,0:T(8,128)} %get-tuple-element.8) | data formatting | bytes 640000

commit v3 on v2

v3 whole, which is shorter than its diff:
```python
import functools

import jax
import jax.numpy as jnp
from jax import lax
from jax.experimental import pallas as pl
from jax.experimental.pallas import tpu as pltpu
from jax.sharding import PartitionSpec as P

MESH = pl.DeviceIdType.MESH
WIDTHS = (256, 256, 256, 128, 128)
GROUP = 4
LANES = 128
F32 = jnp.float32
BF16 = jnp.bfloat16

ORDER = (
    (4, 0), (4, 1), (3, 1), (-3, 0),
    (3, 0), (-3, 1), (2, 0), (-2, 1),
    (2, 1), (-2, 0), (1, 0), (-1, 1),
    (1, 1), (-1, 0), (0, 0), (0, 1),
)
CHAINS = (
    (1, (0, 4, 6, 10)),
    (-1, (1, 5, 7, 11)),
    (1, (2, 8, 12)),
    (-1, (3, 9, 13)),
)
MESSAGES = 14


def nt_dot(left, right):
    return lax.dot_general(
        left, right, (((1,), (1,)), ((), ())), preferred_element_type=F32
    )


def kernel(
    occ_size, aux_size, partner, counts, occ_energy, energies, ao, coef,
    amp_out, orb_out,
    coef_raw, coef_t, own_proj, sums, parcel, landed, scale, amp, gift, gifts, *rest,
):
    windows = rest[:len(WIDTHS)]
    (
        local_sem, ao_send, ao_recv, chain_send, chain_recv, amp_sem,
        gift_send, gift_recv,
    ) = rest[len(WIDTHS):]
    starts = [sum(WIDTHS[:k]) for k in range(len(WIDTHS))]
    occ_me, aux_me = lax.axis_index("occ"), lax.axis_index("aux")
    right = lax.rem(occ_me + 1, occ_size)
    left = lax.rem(occ_me + occ_size - 1, occ_size)
    orbs = ao.shape[0]
    virtuals = ao.shape[1]
    pairs, pnos, _ = coef.shape
    per_orbital = pairs // orbs
    padded = own_proj.shape[1]
    rows = -(-pnos // 16) * 16
    over = pnos - LANES

    def aux_at(distance):
        return lax.rem(aux_me + distance + aux_size, aux_size)

    barrier = pltpu.get_barrier_semaphore()
    for place in ((left, aux_me), (right, aux_me), (occ_me, aux_at(1)), (occ_me, aux_at(-1))):
        pl.semaphore_signal(barrier, inc=1, device_id=place, device_id_type=MESH)

    fetch_coef = pltpu.make_async_copy(coef, coef_raw, local_sem.at[len(WIDTHS)])
    fetch_coef.start()
    fetches = []
    for k, (start, width) in enumerate(zip(starts, WIDTHS)):
        fetch = pltpu.make_async_copy(
            ao.at[:, :, pl.ds(start, width)],
            windows[k].at[pl.ds(orbs, orbs)],
            local_sem.at[k],
        )
        fetch.start()
        fetches.append(fetch)

    pl.semaphore_wait(barrier, 4)

    moves = []
    for k, (start, width) in enumerate(zip(starts, WIDTHS)):
        for side, (target, slot) in enumerate(((right, 0), (left, 2 * orbs))):
            move = pltpu.make_async_remote_copy(
                src_ref=ao.at[:, :, pl.ds(start, width)],
                dst_ref=windows[k].at[pl.ds(slot, orbs)],
                send_sem=ao_send.at[side, k],
                recv_sem=ao_recv.at[side, k],
                device_id=(target, aux_me),
                device_id_type=MESH,
            )
            move.start()
            moves.append(move)

    fetch_coef.wait()
    whole_rows = pnos // 16 * 16
    places = lax.broadcasted_iota(jnp.int32, (pnos, virtuals), 0)

    def mask(s, carry):
        kept = jnp.where(places < counts[s], coef_raw[s].astype(F32), 0.0)
        coef_t[s, whole_rows:] = jnp.zeros((rows - whole_rows, virtuals), BF16)
        coef_t[s, :pnos] = kept.astype(BF16)
        own_proj[s, rows:] = jnp.zeros((padded - rows, own_proj.shape[2]), BF16)
        return carry

    lax.fori_loop(0, pairs, mask, 0)

    first_slot = (occ_me - 1) * orbs

    def slot_of(s):
        return jnp.clip(partner[s] - first_slot, 0, 3 * orbs - 1)

    def own_slot_of(s):
        return orbs + s // per_orbital

    for place in range(2):
        s = 2 * aux_me + place
        shift = occ_energy[first_slot + own_slot_of(s)] + occ_energy[partner[s]]
        row = jnp.broadcast_to(energies[pl.ds(s, 1), :], (pnos, pnos))
        scale[place] = -1.0 / (row + row.T - shift)

    for k, (start, width) in enumerate(zip(starts, WIDTHS)):
        fetches[k].wait()

        def project(o, carry):
            block = windows[k][orbs + o]
            turned = coef_t[pl.ds(o * per_orbital, per_orbital)]
            own = jnp.dot(
                turned.reshape(per_orbital * rows, virtuals), block, preferred_element_type=F32
            )
            own = own.astype(BF16).reshape(per_orbital, rows, width)
            own_proj[pl.ds(o * per_orbital, per_orbital), :rows, start:start + width] = own
            return carry

        lax.fori_loop(0, orbs, project, 0)

    def partials(group, k):
        start, width = starts[k], WIDTHS[k]
        others = [
            jnp.dot(coef_t[s], windows[k][slot_of(s)], preferred_element_type=F32).astype(BF16)
            for s in group
        ]
        owns = [own_proj[s, :, start:start + width] for s in group]
        tops = [nt_dot(own[:rows], other[:LANES]) for own, other in zip(owns, others)]
        rests = [nt_dot(other[LANES:], own) for own, other in zip(owns, others)]
        return [
            jnp.concatenate([top[:pnos], rest[:over, :LANES], rest[:over, LANES:]], axis=0)
            for top, rest in zip(tops, rests)
        ]

    def arrive(k):
        moves[2 * k].wait_recv()
        moves[2 * k + 1].wait_recv()

    last = len(WIDTHS) - 1
    for k in range(last):
        arrive(k)

        def accumulate(number, carry):
            group = [GROUP * number + i for i in range(GROUP)]
            for s, part in zip(group, partials(group, k)):
                sums[s] = part if k == 0 else sums[s] + part
            return carry

        lax.fori_loop(0, pairs // GROUP, accumulate, 0)

    def pair_at(position):
        distance, place = ORDER[position]
        return 2 * aux_at(distance) + place

    messages = {}

    def number_of(chain, step):
        return sum(len(CHAINS[c][1]) for c in range(chain)) + step

    def send(chain, step, total):
        number = number_of(chain, step)
        parcel[number] = total.astype(BF16)
        message = pltpu.make_async_remote_copy(
            src_ref=parcel.at[number],
            dst_ref=landed.at[number],
            send_sem=chain_send.at[number],
            recv_sem=chain_recv.at[number],
            device_id=(occ_me, aux_at(CHAINS[chain][0])),
            device_id_type=MESH,
        )
        message.start()
        messages[chain, step] = message

    def arrived(chain, step):
        messages[chain, step].wait_recv()
        return landed[number_of(chain, step)].astype(F32)

    arrive(last)
    for first in range(0, pairs, GROUP):
        group = [pair_at(position) for position in range(first, first + GROUP)]
        for i, (s, part) in enumerate(zip(group, partials(group, last))):
            total = sums[s] + part
            if first == 0:
                send(i, 0, total)
            else:
                sums[s] = total

    for step in range(1, 4):
        for chain in range(4):
            if step < len(CHAINS[chain][1]):
                s = pair_at(CHAINS[chain][1][step])
                send(chain, step, sums[s] + arrived(chain, step - 1))

    lane = lax.broadcasted_iota(jnp.int32, gift.shape, 1)
    spread = jnp.zeros(gift.shape, F32)
    writes = []

    def added(terms):
        return jnp.sum(jnp.sum(terms, axis=0, keepdims=True), axis=1, keepdims=True)

    for place, (long_chain, short_chain) in enumerate(((0, 3), (1, 2))):
        s = 2 * aux_me + place
        total = sums[s] + arrived(short_chain, 2) + arrived(long_chain, 3)
        low, left_low = total[:LANES], total[LANES:pnos]
        right_up, high = total[pnos:pnos + over], total[pnos + over:, :over]
        scale_low = scale[place, :LANES, :LANES]
        scale_side = scale[place, LANES:, :LANES]
        scale_high = scale[place, LANES:, LANES:]
        amp_low, amp_high = low * scale_low, high * scale_high
        amp[place, :LANES, :LANES] = amp_low
        amp[place, LANES:, :LANES] = left_low * scale_side
        amp[place, :LANES, LANES:] = (right_up * scale_side).T
        amp[place, LANES:, LANES:] = amp_high.T
        write = pltpu.make_async_copy(amp.at[place], amp_out.at[place], amp_sem.at[place])
        write.start()
        writes.append(write)
        mixed = left_low * (left_low - right_up) + right_up * right_up
        energy = 0.5 * (
            added((2.0 * low - low.T) * amp_low)
            + added((2.0 * high - high.T) * amp_high)
            + added(2.0 * mixed * scale_side)
        )
        hits = (lane == own_slot_of(s)).astype(F32) + (lane == slot_of(s)).astype(F32)
        spread = spread + hits * energy

    gift[...] = spread
    gifts[1, aux_me] = spread
    passes = []
    for distance in range(aux_size):
        for side, target in enumerate((right, occ_me, left)):
            if side == 1 and distance == 0:
                continue
            passed = pltpu.make_async_remote_copy(
                src_ref=gift,
                dst_ref=gifts.at[side, aux_me],
                send_sem=gift_send.at[side, distance],
                recv_sem=gift_recv.at[side, distance],
                device_id=(target, aux_at(distance)),
                device_id_type=MESH,
            )
            passed.start()
            passes.append(passed)
    for passed in passes:
        passed.wait_recv()
    from_left, own, from_right = (
        functools.reduce(lambda a, b: a + b, [gifts[side, z] for z in range(aux_size)])
        for side in range(3)
    )
    orb_out[...] = (
        pltpu.roll(from_left, LANES - 2 * orbs, 1)
        + pltpu.roll(own, LANES - orbs, 1)
        + from_right
    )

    for move in moves:
        move.wait_send()
    for message in messages.values():
        message.wait_send()
    for passed in passes:
        passed.wait_send()
    for write in writes:
        write.wait()


def shards(mesh, ao_blocks, pno_coef, pno_energy, occ_energy, pair_partner, pno_count):
    orbs, virtuals, aux_block = ao_blocks.shape
    pairs, _, pnos = pno_coef.shape
    occ_size, aux_size = mesh.shape["occ"], mesh.shape["aux"]
    rows = -(-pnos // 16) * 16
    padded = -(-pnos // LANES) * LANES
    packed = pnos + 2 * (pnos - LANES)
    share = pairs // aux_size
    chunks = len(WIDTHS)
    smem = pl.BlockSpec(memory_space=pltpu.SMEM)
    vmem = pl.BlockSpec(memory_space=pltpu.VMEM)
    anywhere = pl.BlockSpec(memory_space=pl.ANY)
    dma = pltpu.SemaphoreType.DMA
    amplitudes, orbital = pl.pallas_call(
        functools.partial(kernel, occ_size, aux_size),
        out_shape=(
            jax.ShapeDtypeStruct((share, pnos, pnos), F32),
            jax.ShapeDtypeStruct((8, LANES), F32),
        ),
        in_specs=[smem, smem, smem, vmem, anywhere, anywhere],
        out_specs=(anywhere, vmem),
        scratch_shapes=[
            pltpu.VMEM((pairs, pnos, virtuals), BF16),
            pltpu.VMEM((pairs, rows, virtuals), BF16),
            pltpu.VMEM((pairs, padded, aux_block), BF16),
            pltpu.VMEM((pairs, packed, LANES), F32),
            pltpu.VMEM((MESSAGES, packed, LANES), BF16),
            pltpu.VMEM((MESSAGES, packed, LANES), BF16),
            pltpu.VMEM((share, pnos, pnos), F32),
            pltpu.VMEM((share, pnos, pnos), F32),
            pltpu.VMEM((8, LANES), F32),
            pltpu.VMEM((3, aux_size, 8, LANES), F32),
        ]
        + [pltpu.VMEM((3 * orbs, virtuals, width), BF16) for width in WIDTHS]
        + [
            dma((chunks + 1,)),
            dma((2, chunks)),
            dma((2, chunks)),
            dma((MESSAGES,)),
            dma((MESSAGES,)),
            dma((share,)),
            dma((3, aux_size)),
            dma((3, aux_size)),
        ],
        compiler_params=pltpu.CompilerParams(
            collective_id=0, has_side_effects=True, vmem_limit_bytes=53 * 1024 * 1024
        ),
    )(
        pair_partner, pno_count, occ_energy, pno_energy, ao_blocks,
        jnp.swapaxes(pno_coef, 1, 2),
    )
    return amplitudes, orbital[0, :orbs]


def solution(mesh):
    return jax.shard_map(
        functools.partial(shards, mesh),
        mesh=mesh,
        in_specs=(
            P("occ", None, "aux"),
            P("occ", None, None),
            P("occ", None),
            P(),
            P("occ"),
            P("occ"),
        ),
        out_specs=(P(("occ", "aux"), None, None), P("occ")),
        check_vma=False,
    )
```

time: 72.3 us -> 68.3 us (0.945)
  Pallas kernels: 68.2 us -> 63.5 us
  local copies, waits for them, and re-layouts: 2.97 us -> 3.96 us
    pallas_call x1, Pallas kernels: 68.2 us -> 63.5 us  [shards(): pl.pallas_call(functools.partial(kernel, occ_size, aux_size), out_shape=(...]
    unnamed x1 -> x9, local copies, waits for them, and re-layouts: 1.78 us -> 3.45 us
where the time goes in v3:
time: 68.3 us; the launch traced here: 68.1 us
  Pallas kernels  63.5 us (93%)
  local copies, waits for them, and re-layouts  3.96 us (6%)
    pallas_call x1, Pallas kernels, shards(): pl.pallas_call(functools.partial(kernel, occ_size, aux_size), out_shape=(...  63.5 us
    unnamed x9, local copies, waits for them, and re-layouts  3.45 us

profile of v3, /device:TPU:1, one launch (start us, length us, event | category | flops | bytes accessed | tf_op | source)
XLA Modules:
  0.0 68.1 jit_solution(9594529760909630477)
XLA Ops:
  0.6 0.0 copy-start
  0.6 0.7 %copy-done = f32[16,200]{1,0:T(8,128)S(1)} copy-done((f32[16,200]{1,0:T(8,128)S(1)}, f32[16,200]{1,0:T(8,128)}, u32[]{:S(2)}) %copy-start) | copy-done | bytes 12824
  1.4 0.0 copy-start.1
  1.4 0.7 copy-done.1
  2.0 0.0 copy-start.2
  2.0 0.7 copy-done.2
  2.7 0.0 copy-start.3
  2.7 0.7 copy-done.3
  3.3 63.5 %shard_map.77 = (f32[2,200,200]{2,1,0:T(8,128)S(1)}, f32[8,128]{1,0:T(8,128)S(1)}) custom-call(s32[16]{0:T(128)S(1)} %copy-done.2, s32[16]{0:T(128)S(1)} %copy-done.3, f32[256]{0:T(256)S(1)} %copy-done.1, f32[16,200]{1,0:T(8,128)S(1)} %copy-done, bf16[4,256,1024]{2,1,0:T(8,128)(2,1)} %ao.1, bf16[16,200,256]{2,1,0:T(8,128)(2,1)} %bitcast.3), custom_call_target="tpu_custom_call" | custom-call | tf_op jit(solution)/shard_map/pallas_call | solution.py:294
  66.9 0.5 slice_bitcast_fusion
  67.4 0.8 %copy.9 = f32[2,200,200]{2,1,0:T(8,128)} copy(f32[2,200,200]{2,1,0:T(8,128)S(1)} %get-tuple-element.8) | data formatting | bytes 640000
Async XLA Ops:
  0.6 0.7 %copy-start = (f32[16,200]{1,0:T(8,128)S(1)}, f32[16,200]{1,0:T(8,128)}, u32[]{:S(2)}) copy-start(f32[16,200]{1,0:T(8,128)} %energies.1) | copy-start | bytes 38404
  1.4 0.7 copy-start.1
  2.0 0.7 copy-start.2
  2.7 0.7 copy-start.3

commit v4 on v3

--- a/solution.py
+++ b/solution.py
@@ -36,13 +36,13 @@
 
 
 def kernel(
-    occ_size, aux_size, partner, counts, occ_energy, energies, ao, coef,
-    amp_out, orb_out,
-    coef_raw, coef_t, own_proj, sums, parcel, landed, scale, amp, gift, gifts, *rest,
+    occ_size, aux_size, partner_in, counts_in, occ_energy_in, energies_in, ao, coef,
+    amp, orb_out,
+    partner, counts, occ_energy, energies, coef_raw, coef_t, own_proj, sums, parcel, landed, scale, gift, gifts, *rest,
 ):
     windows = rest[:len(WIDTHS)]
     (
-        local_sem, ao_send, ao_recv, chain_send, chain_recv, amp_sem,
+        small_sem, local_sem, ao_send, ao_recv, chain_send, chain_recv,
         gift_send, gift_recv,
     ) = rest[len(WIDTHS):]
     starts = [sum(WIDTHS[:k]) for k in range(len(WIDTHS))]
@@ -64,18 +64,6 @@
     for place in ((left, aux_me), (right, aux_me), (occ_me, aux_at(1)), (occ_me, aux_at(-1))):
         pl.semaphore_signal(barrier, inc=1, device_id=place, device_id_type=MESH)
 
-    fetch_coef = pltpu.make_async_copy(coef, coef_raw, local_sem.at[len(WIDTHS)])
-    fetch_coef.start()
-    fetches = []
-    for k, (start, width) in enumerate(zip(starts, WIDTHS)):
-        fetch = pltpu.make_async_copy(
-            ao.at[:, :, pl.ds(start, width)],
-            windows[k].at[pl.ds(orbs, orbs)],
-            local_sem.at[k],
-        )
-        fetch.start()
-        fetches.append(fetch)
-
     pl.semaphore_wait(barrier, 4)
 
     moves = []
@@ -92,7 +80,26 @@
             move.start()
             moves.append(move)
 
-    fetch_coef.wait()
+    smalls = []
+    for number, (source, target) in enumerate((
+        (counts_in, counts), (partner_in, partner), (occ_energy_in, occ_energy),
+        (energies_in, energies), (coef, coef_raw),
+    )):
+        small = pltpu.make_async_copy(source, target, small_sem.at[number])
+        small.start()
+        smalls.append(small)
+    fetches = []
+    for k, (start, width) in enumerate(zip(starts, WIDTHS)):
+        fetch = pltpu.make_async_copy(
+            ao.at[:, :, pl.ds(start, width)],
+            windows[k].at[pl.ds(orbs, orbs)],
+            local_sem.at[k],
+        )
+        fetch.start()
+        fetches.append(fetch)
+
+    for small in smalls:
+        small.wait()
     whole_rows = pnos // 16 * 16
     places = lax.broadcasted_iota(jnp.int32, (pnos, virtuals), 0)
 
@@ -173,67 +180,73 @@
     def number_of(chain, step):
         return sum(len(CHAINS[c][1]) for c in range(chain)) + step
 
-    def send(chain, step, total):
+    packed = sums.shape[1]
+    middle = -(-packed // 32) * 16
+    halves = (pl.ds(0, middle), pl.ds(middle, packed - middle))
+
+    def send(chain, step, half, total):
         number = number_of(chain, step)
-        parcel[number] = total.astype(BF16)
+        parcel[number, halves[half]] = total.astype(BF16)
         message = pltpu.make_async_remote_copy(
-            src_ref=parcel.at[number],
-            dst_ref=landed.at[number],
-            send_sem=chain_send.at[number],
-            recv_sem=chain_recv.at[number],
+            src_ref=parcel.at[number, halves[half]],
+            dst_ref=landed.at[number, halves[half]],
+            send_sem=chain_send.at[number, half],
+            recv_sem=chain_recv.at[number, half],
             device_id=(occ_me, aux_at(CHAINS[chain][0])),
             device_id_type=MESH,
         )
         message.start()
-        messages[chain, step] = message
-
-    def arrived(chain, step):
-        messages[chain, step].wait_recv()
-        return landed[number_of(chain, step)].astype(F32)
+        messages[chain, step, half] = message
+
+    def arrived(chain, step, half):
+        messages[chain, step, half].wait_recv()
+        return landed[number_of(chain, step), halves[half]].astype(F32)
 
     arrive(last)
     for first in range(0, pairs, GROUP):
         group = [pair_at(position) for position in range(first, first + GROUP)]
-        for i, (s, part) in enumerate(zip(group, partials(group, last))):
-            total = sums[s] + part
-            if first == 0:
-                send(i, 0, total)
-            else:
+        totals = [sums[s] + part for s, part in zip(group, partials(group, last))]
+        for s, total in zip(group, totals):
+            if first > 0:
                 sums[s] = total
+        if first == 0:
+            for chains in ((0, 1), (2, 3)):
+                for half, part in enumerate((slice(0, middle), slice(middle, packed))):
+                    for chain in chains:
+                        send(chain, 0, half, totals[chain][part])
 
     for step in range(1, 4):
-        for chain in range(4):
-            if step < len(CHAINS[chain][1]):
-                s = pair_at(CHAINS[chain][1][step])
-                send(chain, step, sums[s] + arrived(chain, step - 1))
+        for chains in ((0, 1), (2, 3)):
+            for half in range(2):
+                for chain in chains:
+                    if step < len(CHAINS[chain][1]):
+                        s = pair_at(CHAINS[chain][1][step])
+                        send(chain, step, half, sums[s, halves[half]] + arrived(chain, step - 1, half))
 
     lane = lax.broadcasted_iota(jnp.int32, gift.shape, 1)
     spread = jnp.zeros(gift.shape, F32)
-    writes = []
 
     def added(terms):
         return jnp.sum(jnp.sum(terms, axis=0, keepdims=True), axis=1, keepdims=True)
 
+    def scales(place):
+        return (
+            scale[place, :LANES, :LANES], scale[place, LANES:, :LANES], scale[place, LANES:, LANES:]
+        )
+
     for place, (long_chain, short_chain) in enumerate(((0, 3), (1, 2))):
         s = 2 * aux_me + place
-        total = sums[s] + arrived(short_chain, 2) + arrived(long_chain, 3)
-        low, left_low = total[:LANES], total[LANES:pnos]
-        right_up, high = total[pnos:pnos + over], total[pnos + over:, :over]
-        scale_low = scale[place, :LANES, :LANES]
-        scale_side = scale[place, LANES:, :LANES]
-        scale_high = scale[place, LANES:, LANES:]
-        amp_low, amp_high = low * scale_low, high * scale_high
-        amp[place, :LANES, :LANES] = amp_low
-        amp[place, LANES:, :LANES] = left_low * scale_side
-        amp[place, :LANES, LANES:] = (right_up * scale_side).T
-        amp[place, LANES:, LANES:] = amp_high.T
-        write = pltpu.make_async_copy(amp.at[place], amp_out.at[place], amp_sem.at[place])
-        write.start()
-        writes.append(write)
+        for half in range(2):
+            sums[s, halves[half]] = (
+                sums[s, halves[half]] + arrived(short_chain, 2, half) + arrived(long_chain, 3, half)
+            )
+        low, left_low = sums[s, :LANES], sums[s, LANES:pnos]
+        right_up, high = sums[s, pnos:pnos + over], sums[s, pnos + over:, :over]
+        scale_low, scale_side, scale_high = scales(place)
         mixed = left_low * (left_low - right_up) + right_up * right_up
         energy = 0.5 * (
-            added((2.0 * low - low.T) * amp_low)
-            + added((2.0 * high - high.T) * amp_high)
+            added((2.0 * low - low.T) * low * scale_low)
+            + added((2.0 * high - high.T) * high * scale_high)
             + added(2.0 * mixed * scale_side)
         )
         hits = (lane == own_slot_of(s)).astype(F32) + (lane == slot_of(s)).astype(F32)
@@ -256,6 +269,15 @@
             )
             passed.start()
             passes.append(passed)
+
+    for place in range(2):
+        s = 2 * aux_me + place
+        scale_low, scale_side, scale_high = scales(place)
+        amp[place, :LANES, :LANES] = sums[s, :LANES] * scale_low
+        amp[place, LANES:, :LANES] = sums[s, LANES:pnos] * scale_side
+        amp[place, :LANES, LANES:] = (sums[s, pnos:pnos + over] * scale_side).T
+        amp[place, LANES:, LANES:] = (sums[s, pnos + over:, :over] * scale_high).T
+
     for passed in passes:
         passed.wait_recv()
     from_left, own, from_right = (
@@ -274,8 +296,6 @@
         message.wait_send()
     for passed in passes:
         passed.wait_send()
-    for write in writes:
-        write.wait()
 
 
 def shards(mesh, ao_blocks, pno_coef, pno_energy, occ_energy, pair_partner, pno_count):
@@ -287,7 +307,6 @@
     packed = pnos + 2 * (pnos - LANES)
     share = pairs // aux_size
     chunks = len(WIDTHS)
-    smem = pl.BlockSpec(memory_space=pltpu.SMEM)
     vmem = pl.BlockSpec(memory_space=pltpu.VMEM)
     anywhere = pl.BlockSpec(memory_space=pl.ANY)
     dma = pltpu.SemaphoreType.DMA
@@ -297,9 +316,13 @@
             jax.ShapeDtypeStruct((share, pnos, pnos), F32),
             jax.ShapeDtypeStruct((8, LANES), F32),
         ),
-        in_specs=[smem, smem, smem, vmem, anywhere, anywhere],
-        out_specs=(anywhere, vmem),
+        in_specs=[anywhere] * 6,
+        out_specs=(vmem, vmem),
         scratch_shapes=[
+            pltpu.SMEM((pairs,), jnp.int32),
+            pltpu.SMEM((pairs,), jnp.int32),
+            pltpu.SMEM(occ_energy.shape, F32),
+            pltpu.VMEM((pairs, pnos), F32),
             pltpu.VMEM((pairs, pnos, virtuals), BF16),
             pltpu.VMEM((pairs, rows, virtuals), BF16),
             pltpu.VMEM((pairs, padded, aux_block), BF16),
@@ -307,27 +330,31 @@
             pltpu.VMEM((MESSAGES, packed, LANES), BF16),
             pltpu.VMEM((MESSAGES, packed, LANES), BF16),
             pltpu.VMEM((share, pnos, pnos), F32),
-            pltpu.VMEM((share, pnos, pnos), F32),
             pltpu.VMEM((8, LANES), F32),
             pltpu.VMEM((3, aux_size, 8, LANES), F32),
         ]
         + [pltpu.VMEM((3 * orbs, virtuals, width), BF16) for width in WIDTHS]
         + [
-            dma((chunks + 1,)),
+            dma((5,)),
+            dma((chunks,)),
             dma((2, chunks)),
             dma((2, chunks)),
-            dma((MESSAGES,)),
-            dma((MESSAGES,)),
-            dma((share,)),
+            dma((MESSAGES, 2)),
+            dma((MESSAGES, 2)),
             dma((3, aux_size)),
             dma((3, aux_size)),
         ],
         compiler_params=pltpu.CompilerParams(
-            collective_id=0, has_side_effects=True, vmem_limit_bytes=53 * 1024 * 1024
+            collective_id=0, has_side_effects=True, vmem_limit_bytes=48 * 1024 * 1024
         ),
     )(
-        pair_partner, pno_count, occ_energy, pno_energy, ao_blocks,
-        jnp.swapaxes(pno_coef, 1, 2),
+        *(
+            pltpu.with_memory_space_constraint(x, pltpu.HBM)
+            for x in (
+                pair_partner, pno_count, occ_energy, pno_energy, ao_blocks,
+                jnp.swapaxes(pno_coef, 1, 2),
+            )
+        )
     )
     return amplitudes, orbital[0, :orbs]
 

time: 68.3 us -> 63 us (0.922)
  local copies, waits for them, and re-layouts: 3.96 us -> 1.26 us
  Pallas kernels: 63.5 us -> 61 us
    unnamed x9 -> x1, local copies, waits for them, and re-layouts: 3.45 us -> 0.75 us
    pallas_call x1, Pallas kernels: 63.5 us -> 61 us  [shards(): pl.pallas_call(functools.partial(kernel, occ_size, aux_size), out_shape=(...]
where the time goes in v4:
time: 63 us; the launch traced here: 62.9 us
  Pallas kernels  61 us (97%)
  local copies, waits for them, and re-layouts  1.26 us (2%)
  between operations  0.64 us (1%)
    pallas_call x1, Pallas kernels, shards(): pl.pallas_call(functools.partial(kernel, occ_size, aux_size), out_shape=(...  61 us

profile of v4, /device:TPU:1, one launch (start us, length us, event | category | flops | bytes accessed | tf_op | source)
XLA Modules:
  0.0 62.9 jit_solution(5344848261899751574)
XLA Ops:
  0.6 61.0 %shard_map.77 = (f32[2,200,200]{2,1,0:T(8,128)S(1)}, f32[8,128]{1,0:T(8,128)S(1)}) custom-call(s32[16]{0:T(128)} %partner_in.1, s32[16]{0:T(128)} %counts_in.1, f32[256]{0:T(256)} %occ_energy_in.1, f32[16,200]{1,0:T(8,128)} %energies_in.1, bf16[4,256,1024]{2,1,0:T(8,128)(2,1)} %ao.1, bf16[16,200,256]{2,1,0:T(8,128)(2,1)} %bitcast.3), custom_call_target="tpu_custom_call" | custom-call | tf_op jit(solution)/shard_map/pallas_call | solution.py:313
  61.6 0.5 slice_bitcast_fusion
  62.2 0.8 %copy.9 = f32[2,200,200]{2,1,0:T(8,128)} copy(f32[2,200,200]{2,1,0:T(8,128)S(1)} %get-tuple-element.8) | data formatting | bytes 640000

commit v5 on v4

--- a/solution.py
+++ b/solution.py
@@ -38,7 +38,7 @@
 def kernel(
     occ_size, aux_size, partner_in, counts_in, occ_energy_in, energies_in, ao, coef,
     amp, orb_out,
-    partner, counts, occ_energy, energies, coef_raw, coef_t, own_proj, sums, parcel, landed, scale, gift, gifts, *rest,
+    partner, counts, occ_energy, energies, coef_raw, coef_t, own_proj, sums, parcel, landed, scale, corners, gift, gifts, *rest,
 ):
     windows = rest[:len(WIDTHS)]
     (
@@ -56,6 +56,9 @@
     padded = own_proj.shape[1]
     rows = -(-pnos // 16) * 16
     over = pnos - LANES
+    fold, tail = LANES // 2, pnos + over
+    strip = over - fold
+    low_lanes = lax.broadcasted_iota(jnp.int32, (fold // 2, LANES), 1) < fold
 
     def aux_at(distance):
         return lax.rem(aux_me + distance + aux_size, aux_size)
@@ -72,7 +75,7 @@
             move = pltpu.make_async_remote_copy(
                 src_ref=ao.at[:, :, pl.ds(start, width)],
                 dst_ref=windows[k].at[pl.ds(slot, orbs)],
-                send_sem=ao_send.at[side, k],
+                send_sem=ao_send.at[side],
                 recv_sem=ao_recv.at[side, k],
                 device_id=(target, aux_me),
                 device_id_type=MESH,
@@ -141,6 +144,23 @@
 
         lax.fori_loop(0, orbs, project, 0)
 
+    def pack(top, rest, strip_rows):
+        corner = rest[:, LANES:]
+        folded = jnp.where(
+            low_lanes, corner[:fold // 2], pltpu.roll(corner[fold // 2:fold], fold, 1)
+        )
+        return jnp.concatenate(
+            [top[:pnos], rest[:over, :LANES], folded, corner[fold:over], strip_rows[16 - (rows - pnos) - strip:16 - (rows - pnos)]],
+            axis=0,
+        )
+
+    def unpack_corner(low_rows, last_rows, strip_rows):
+        turned = jnp.concatenate(
+            [low_rows, pltpu.roll(low_rows, fold, 1), last_rows], axis=0
+        ).T
+        bottom = pltpu.roll(strip_rows, LANES - (LANES - rows + LANES), 1)
+        return jnp.concatenate([turned[:fold], bottom[:, :over]], axis=0)
+
     def partials(group, k):
         start, width = starts[k], WIDTHS[k]
         others = [
@@ -150,10 +170,8 @@
         owns = [own_proj[s, :, start:start + width] for s in group]
         tops = [nt_dot(own[:rows], other[:LANES]) for own, other in zip(owns, others)]
         rests = [nt_dot(other[LANES:], own) for own, other in zip(owns, others)]
-        return [
-            jnp.concatenate([top[:pnos], rest[:over, :LANES], rest[:over, LANES:]], axis=0)
-            for top, rest in zip(tops, rests)
-        ]
+        strips = [nt_dot(own[rows - 16:rows], other[rows - LANES:]) for own, other in zip(owns, others)]
+        return [pack(*terms) for terms in zip(tops, rests, strips)]
 
     def arrive(k):
         moves[2 * k].wait_recv()
@@ -190,7 +208,7 @@
         message = pltpu.make_async_remote_copy(
             src_ref=parcel.at[number, halves[half]],
             dst_ref=landed.at[number, halves[half]],
-            send_sem=chain_send.at[number, half],
+            send_sem=chain_send,
             recv_sem=chain_recv.at[number, half],
             device_id=(occ_me, aux_at(CHAINS[chain][0])),
             device_id_type=MESH,
@@ -240,8 +258,13 @@
             sums[s, halves[half]] = (
                 sums[s, halves[half]] + arrived(short_chain, 2, half) + arrived(long_chain, 3, half)
             )
-        low, left_low = sums[s, :LANES], sums[s, LANES:pnos]
-        right_up, high = sums[s, pnos:pnos + over], sums[s, pnos + over:, :over]
+        low, left_low, right_up = sums[s, :LANES], sums[s, LANES:pnos], sums[s, pnos:tail]
+        high = unpack_corner(
+            sums[s, tail:tail + fold // 2],
+            sums[s, tail + fold // 2:tail + fold // 2 + strip],
+            sums[s, tail + fold // 2 + strip:],
+        )
+        corners[place] = high
         scale_low, scale_side, scale_high = scales(place)
         mixed = left_low * (left_low - right_up) + right_up * right_up
         energy = 0.5 * (
@@ -253,35 +276,41 @@
         spread = spread + hits * energy
 
     gift[...] = spread
-    gifts[1, aux_me] = spread
-    passes = []
+    gifts[aux_size + aux_me] = spread
     for distance in range(aux_size):
         for side, target in enumerate((right, occ_me, left)):
             if side == 1 and distance == 0:
                 continue
             passed = pltpu.make_async_remote_copy(
                 src_ref=gift,
-                dst_ref=gifts.at[side, aux_me],
-                send_sem=gift_send.at[side, distance],
-                recv_sem=gift_recv.at[side, distance],
+                dst_ref=gifts.at[side * aux_size + aux_me],
+                send_sem=gift_send,
+                recv_sem=gift_recv,
                 device_id=(target, aux_at(distance)),
                 device_id_type=MESH,
             )
             passed.start()
-            passes.append(passed)
+    others = gifts.at[pl.ds(0, 3 * aux_size - 1)]
+    all_passed = pltpu.make_async_remote_copy(
+        src_ref=others,
+        dst_ref=others,
+        send_sem=gift_send,
+        recv_sem=gift_recv,
+        device_id=(right, aux_me),
+        device_id_type=MESH,
+    )
 
     for place in range(2):
         s = 2 * aux_me + place
         scale_low, scale_side, scale_high = scales(place)
         amp[place, :LANES, :LANES] = sums[s, :LANES] * scale_low
         amp[place, LANES:, :LANES] = sums[s, LANES:pnos] * scale_side
-        amp[place, :LANES, LANES:] = (sums[s, pnos:pnos + over] * scale_side).T
-        amp[place, LANES:, LANES:] = (sums[s, pnos + over:, :over] * scale_high).T
-
-    for passed in passes:
-        passed.wait_recv()
+        amp[place, :LANES, LANES:] = (sums[s, pnos:tail] * scale_side).T
+        amp[place, LANES:, LANES:] = corners[place] * scale_high
+
+    all_passed.wait_recv()
     from_left, own, from_right = (
-        functools.reduce(lambda a, b: a + b, [gifts[side, z] for z in range(aux_size)])
+        functools.reduce(lambda a, b: a + b, [gifts[side * aux_size + z] for z in range(aux_size)])
         for side in range(3)
     )
     orb_out[...] = (
@@ -290,12 +319,24 @@
         + from_right
     )
 
-    for move in moves:
-        move.wait_send()
-    for message in messages.values():
-        message.wait_send()
-    for passed in passes:
-        passed.wait_send()
+    for side in range(2):
+        pltpu.make_async_remote_copy(
+            src_ref=ao,
+            dst_ref=ao,
+            send_sem=ao_send.at[side],
+            recv_sem=ao_recv.at[side, 0],
+            device_id=(right, aux_me),
+            device_id_type=MESH,
+        ).wait_send()
+    pltpu.make_async_remote_copy(
+        src_ref=parcel,
+        dst_ref=landed,
+        send_sem=chain_send,
+        recv_sem=chain_recv.at[0, 0],
+        device_id=(right, aux_me),
+        device_id_type=MESH,
+    ).wait_send()
+    all_passed.wait_send()
 
 
 def shards(mesh, ao_blocks, pno_coef, pno_energy, occ_energy, pair_partner, pno_count):
@@ -304,7 +345,7 @@
     occ_size, aux_size = mesh.shape["occ"], mesh.shape["aux"]
     rows = -(-pnos // 16) * 16
     padded = -(-pnos // LANES) * LANES
-    packed = pnos + 2 * (pnos - LANES)
+    packed = pnos + (pnos - LANES) + LANES // 4 + 2 * (pnos - LANES - LANES // 2)
     share = pairs // aux_size
     chunks = len(WIDTHS)
     vmem = pl.BlockSpec(memory_space=pltpu.VMEM)
@@ -330,19 +371,20 @@
             pltpu.VMEM((MESSAGES, packed, LANES), BF16),
             pltpu.VMEM((MESSAGES, packed, LANES), BF16),
             pltpu.VMEM((share, pnos, pnos), F32),
+            pltpu.VMEM((share, pnos - LANES, pnos - LANES), F32),
             pltpu.VMEM((8, LANES), F32),
-            pltpu.VMEM((3, aux_size, 8, LANES), F32),
+            pltpu.VMEM((3 * aux_size, 8, LANES), F32),
         ]
         + [pltpu.VMEM((3 * orbs, virtuals, width), BF16) for width in WIDTHS]
         + [
             dma((5,)),
             dma((chunks,)),
+            dma((2,)),
             dma((2, chunks)),
-            dma((2, chunks)),
+            dma,
             dma((MESSAGES, 2)),
-            dma((MESSAGES, 2)),
-            dma((3, aux_size)),
-            dma((3, aux_size)),
+            dma,
+            dma,
         ],
         compiler_params=pltpu.CompilerParams(
             collective_id=0, has_side_effects=True, vmem_limit_bytes=48 * 1024 * 1024

time: 63 us -> 61.8 us (0.981)
  Pallas kernels: 61 us -> 59.8 us
    pallas_call x1, Pallas kernels: 61 us -> 59.8 us  [shards(): pl.pallas_call(functools.partial(kernel, occ_size, aux_size), out_shape=(...]
where the time goes in v5:
time: 61.8 us; the launch traced here: 61.7 us
  Pallas kernels  59.8 us (97%)
  local copies, waits for them, and re-layouts  1.26 us (2%)
  between operations  0.64 us (1%)
    pallas_call x1, Pallas kernels, shards(): pl.pallas_call(functools.partial(kernel, occ_size, aux_size), out_shape=(...  59.8 us

profile of v5, /device:TPU:1, one launch (start us, length us, event | category | flops | bytes accessed | tf_op | source)
XLA Modules:
  0.0 61.7 jit_solution(10195470638744937733)
XLA Ops:
  0.6 59.8 %shard_map.77 = (f32[2,200,200]{2,1,0:T(8,128)S(1)}, f32[8,128]{1,0:T(8,128)S(1)}) custom-call(s32[16]{0:T(128)} %partner_in.1, s32[16]{0:T(128)} %counts_in.1, f32[256]{0:T(256)} %occ_energy_in.1, f32[16,200]{1,0:T(8,128)} %energies_in.1, bf16[4,256,1024]{2,1,0:T(8,128)(2,1)} %ao.1, bf16[16,200,256]{2,1,0:T(8,128)(2,1)} %bitcast.3), custom_call_target="tpu_custom_call" | custom-call | tf_op jit(solution)/shard_map/pallas_call | solution.py:354
  60.4 0.5 slice_bitcast_fusion
  60.9 0.8 %copy.9 = f32[2,200,200]{2,1,0:T(8,128)} copy(f32[2,200,200]{2,1,0:T(8,128)S(1)} %get-tuple-element.8) | data formatting | bytes 640000

commit v6 on v5

--- a/solution.py
+++ b/solution.py
@@ -43,7 +43,7 @@
     windows = rest[:len(WIDTHS)]
     (
         small_sem, local_sem, ao_send, ao_recv, chain_send, chain_recv,
-        gift_send, gift_recv,
+        gift_send, gift_recv, ready,
     ) = rest[len(WIDTHS):]
     starts = [sum(WIDTHS[:k]) for k in range(len(WIDTHS))]
     occ_me, aux_me = lax.axis_index("occ"), lax.axis_index("aux")
@@ -63,11 +63,28 @@
     def aux_at(distance):
         return lax.rem(aux_me + distance + aux_size, aux_size)
 
+    top = aux_size - 1
+    first_occ, last_occ = occ_me == 0, occ_me == occ_size - 1
     barrier = pltpu.get_barrier_semaphore()
-    for place in ((left, aux_me), (right, aux_me), (occ_me, aux_at(1)), (occ_me, aux_at(-1))):
-        pl.semaphore_signal(barrier, inc=1, device_id=place, device_id_type=MESH)
-
-    pl.semaphore_wait(barrier, 4)
+
+    def announce(semaphore, occ_place, aux_place):
+        pl.semaphore_signal(
+            semaphore, inc=1, device_id=(occ_place, aux_place), device_id_type=MESH
+        )
+
+    pl.when(jnp.logical_not(first_occ))(lambda: announce(barrier, left, aux_me))
+    pl.when(jnp.logical_not(last_occ))(lambda: announce(barrier, right, aux_me))
+
+    @pl.when(aux_me < top)
+    def _():
+        announce(barrier, occ_me, aux_at(1))
+
+    @pl.when(aux_me == 0)
+    def _():
+        announce(barrier, occ_me, aux_at(-1))
+
+    beside = (occ_me + occ_size - 1) // occ_size + (2 * occ_size - 2 - occ_me) // occ_size
+    pl.semaphore_wait(barrier, beside + (aux_me + top) // aux_size + aux_me // top)
 
     moves = []
     for k, (start, width) in enumerate(zip(starts, WIDTHS)):
@@ -80,8 +97,23 @@
                 device_id=(target, aux_me),
                 device_id_type=MESH,
             )
-            move.start()
             moves.append(move)
+            stand_in = pltpu.make_async_copy(
+                ao.at[:, :, pl.ds(start, width)],
+                windows[k].at[pl.ds(slot, orbs)],
+                ao_recv.at[side, k],
+            )
+            goes, lacks = ((last_occ, first_occ), (first_occ, last_occ))[side]
+            pl.when(jnp.logical_not(goes))(move.start)
+            pl.when(lacks)(stand_in.start)
+
+    @pl.when(aux_me > 0)
+    def _():
+        announce(ready, occ_me, aux_at(-1))
+
+    @pl.when(aux_me == top)
+    def _():
+        announce(ready, occ_me, aux_at(1))
 
     smalls = []
     for number, (source, target) in enumerate((
@@ -106,6 +138,12 @@
     whole_rows = pnos // 16 * 16
     places = lax.broadcasted_iota(jnp.int32, (pnos, virtuals), 0)
 
+    for side, lacks in ((0, first_occ), (2, last_occ)):
+        @pl.when(lacks)
+        def _():
+            for z in range(aux_size):
+                gifts[side * aux_size + z] = jnp.zeros(gift.shape, F32)
+
     def mask(s, carry):
         kept = jnp.where(places < counts[s], coef_raw[s].astype(F32), 0.0)
         coef_t[s, whole_rows:] = jnp.zeros((rows - whole_rows, virtuals), BF16)
@@ -219,6 +257,14 @@
     def arrived(chain, step, half):
         messages[chain, step, half].wait_recv()
         return landed[number_of(chain, step), halves[half]].astype(F32)
+
+    @pl.when(jnp.logical_and(aux_me > 0, aux_me < top))
+    def _():
+        pl.semaphore_wait(ready, 1)
+
+    @pl.when(aux_me == 0)
+    def _():
+        pl.semaphore_wait(ready, 2)
 
     arrive(last)
     for first in range(0, pairs, GROUP):
@@ -277,6 +323,15 @@
 
     gift[...] = spread
     gifts[aux_size + aux_me] = spread
+    lacking = (first_occ, None, last_occ)
+    barred = (last_occ, None, first_occ)
+
+    def unless(condition, action):
+        if condition is None:
+            action()
+        else:
+            pl.when(jnp.logical_not(condition))(action)
+
     for distance in range(aux_size):
         for side, target in enumerate((right, occ_me, left)):
             if side == 1 and distance == 0:
@@ -284,21 +339,25 @@
             passed = pltpu.make_async_remote_copy(
                 src_ref=gift,
                 dst_ref=gifts.at[side * aux_size + aux_me],
-                send_sem=gift_send,
-                recv_sem=gift_recv,
+                send_sem=gift_send.at[side],
+                recv_sem=gift_recv.at[side],
                 device_id=(target, aux_at(distance)),
                 device_id_type=MESH,
             )
-            passed.start()
-    others = gifts.at[pl.ds(0, 3 * aux_size - 1)]
-    all_passed = pltpu.make_async_remote_copy(
-        src_ref=others,
-        dst_ref=others,
-        send_sem=gift_send,
-        recv_sem=gift_recv,
-        device_id=(right, aux_me),
-        device_id_type=MESH,
-    )
+            unless(barred[side], passed.start)
+    passes = []
+    for side in range(3):
+        several = gifts.at[pl.ds(0, aux_size - (side == 1))]
+        passes.append(
+            pltpu.make_async_remote_copy(
+                src_ref=several,
+                dst_ref=several,
+                send_sem=gift_send.at[side],
+                recv_sem=gift_recv.at[side],
+                device_id=(right, aux_me),
+                device_id_type=MESH,
+            )
+        )
 
     for place in range(2):
         s = 2 * aux_me + place
@@ -308,7 +367,8 @@
         amp[place, :LANES, LANES:] = (sums[s, pnos:tail] * scale_side).T
         amp[place, LANES:, LANES:] = corners[place] * scale_high
 
-    all_passed.wait_recv()
+    for side, passed in enumerate(passes):
+        unless(lacking[side], passed.wait_recv)
     from_left, own, from_right = (
         functools.reduce(lambda a, b: a + b, [gifts[side * aux_size + z] for z in range(aux_size)])
         for side in range(3)
@@ -319,15 +379,16 @@
         + from_right
     )
 
-    for side in range(2):
-        pltpu.make_async_remote_copy(
+    for side, goes in enumerate((last_occ, first_occ)):
+        moved = pltpu.make_async_remote_copy(
             src_ref=ao,
             dst_ref=ao,
             send_sem=ao_send.at[side],
             recv_sem=ao_recv.at[side, 0],
             device_id=(right, aux_me),
             device_id_type=MESH,
-        ).wait_send()
+        )
+        unless(goes, moved.wait_send)
     pltpu.make_async_remote_copy(
         src_ref=parcel,
         dst_ref=landed,
@@ -336,7 +397,8 @@
         device_id=(right, aux_me),
         device_id_type=MESH,
     ).wait_send()
-    all_passed.wait_send()
+    for side, passed in enumerate(passes):
+        unless(barred[side], passed.wait_send)
 
 
 def shards(mesh, ao_blocks, pno_coef, pno_energy, occ_energy, pair_partner, pno_count):
@@ -383,8 +445,9 @@
             dma((2, chunks)),
             dma,
             dma((MESSAGES, 2)),
-            dma,
-            dma,
+            dma((3,)),
+            dma((3,)),
+            pltpu.SemaphoreType.REGULAR,
         ],
         compiler_params=pltpu.CompilerParams(
             collective_id=0, has_side_effects=True, vmem_limit_bytes=48 * 1024 * 1024

time: 61.8 us -> 59.7 us (0.966)
  the two profiles are of different devices: /device:TPU:1 before, /device:TPU:29 now
where the time goes in v6:
time: 59.7 us; the launch traced here: 59.6 us
  Pallas kernels  57.7 us (97%)
  local copies, waits for them, and re-layouts  1.26 us (2%)
  between operations  0.64 us (1%)
    pallas_call x1, Pallas kernels, shards(): pl.pallas_call(functools.partial(kernel, occ_size, aux_size), out_shape=(...  57.7 us

profile of v6, /device:TPU:29, one launch (start us, length us, event | category | flops | bytes accessed | tf_op | source)
XLA Modules:
  0.0 59.6 jit_solution(5798552874422564877)
XLA Ops:
  0.6 57.7 %shard_map.77 = (f32[2,200,200]{2,1,0:T(8,128)S(1)}, f32[8,128]{1,0:T(8,128)S(1)}) custom-call(s32[16]{0:T(128)} %partner_in.1, s32[16]{0:T(128)} %counts_in.1, f32[256]{0:T(256)} %occ_energy_in.1, f32[16,200]{1,0:T(8,128)} %energies_in.1, bf16[4,256,1024]{2,1,0:T(8,128)(2,1)} %ao.1, bf16[16,200,256]{2,1,0:T(8,128)(2,1)} %bitcast.3), custom_call_target="tpu_custom_call" | custom-call | tf_op jit(solution)/shard_map/pallas_call | solution.py:416
  58.3 0.5 slice_bitcast_fusion
  58.9 0.8 %copy.9 = f32[2,200,200]{2,1,0:T(8,128)} copy(f32[2,200,200]{2,1,0:T(8,128)S(1)} %get-tuple-element.8) | data formatting | bytes 640000

commit v7 on v6

--- a/solution.py
+++ b/solution.py
@@ -8,7 +8,9 @@
 from jax.sharding import PartitionSpec as P
 
 MESH = pl.DeviceIdType.MESH
-WIDTHS = (256, 256, 256, 128, 128)
+WIDTHS = (256, 256, 256, 128, 128, 128)
+FINAL, OWN_LOAN, BORROWED = 3, 4, 5
+LENDERS = 2
 GROUP = 4
 LANES = 128
 F32 = jnp.float32
@@ -42,7 +44,7 @@
 ):
     windows = rest[:len(WIDTHS)]
     (
-        small_sem, local_sem, ao_send, ao_recv, chain_send, chain_recv,
+        small_sem, local_sem, ao_send, ao_recv, loan_sem, chain_send, chain_recv,
         gift_send, gift_recv, ready,
     ) = rest[len(WIDTHS):]
     starts = [sum(WIDTHS[:k]) for k in range(len(WIDTHS))]
@@ -79,33 +81,53 @@
     def _():
         announce(barrier, occ_me, aux_at(1))
 
-    @pl.when(aux_me == 0)
-    def _():
-        announce(barrier, occ_me, aux_at(-1))
+    late, early = aux_me > top - LENDERS, aux_me < LENDERS
+
+    @pl.when(early)
+    def _():
+        announce(barrier, occ_me, top - aux_me)
 
     beside = (occ_me + occ_size - 1) // occ_size + (2 * occ_size - 2 - occ_me) // occ_size
-    pl.semaphore_wait(barrier, beside + (aux_me + top) // aux_size + aux_me // top)
-
-    moves = []
-    for k, (start, width) in enumerate(zip(starts, WIDTHS)):
-        for side, (target, slot) in enumerate(((right, 0), (left, 2 * orbs))):
-            move = pltpu.make_async_remote_copy(
-                src_ref=ao.at[:, :, pl.ds(start, width)],
-                dst_ref=windows[k].at[pl.ds(slot, orbs)],
-                send_sem=ao_send.at[side],
-                recv_sem=ao_recv.at[side, k],
-                device_id=(target, aux_me),
-                device_id_type=MESH,
-            )
-            moves.append(move)
+    pl.semaphore_wait(barrier, beside + (aux_me + top) // aux_size + (aux_me + LENDERS) // aux_size)
+
+    def source_of(k):
+        if k == BORROWED:
+            return windows[k].at[pl.ds(orbs, orbs)]
+        return ao.at[:, :, pl.ds(starts[k], WIDTHS[k])]
+
+    def move(k, side):
+        target, slot = ((right, 0), (left, 2 * orbs))[side]
+        return pltpu.make_async_remote_copy(
+            src_ref=source_of(k),
+            dst_ref=windows[k].at[pl.ds(slot, orbs)],
+            send_sem=ao_send.at[side, max(k, FINAL) - FINAL],
+            recv_sem=ao_recv.at[side, k],
+            device_id=(target, aux_me),
+            device_id_type=MESH,
+        )
+
+    def start_moves(k):
+        for side, slot in enumerate((0, 2 * orbs)):
             stand_in = pltpu.make_async_copy(
-                ao.at[:, :, pl.ds(start, width)],
-                windows[k].at[pl.ds(slot, orbs)],
-                ao_recv.at[side, k],
+                source_of(k), windows[k].at[pl.ds(slot, orbs)], ao_recv.at[side, k]
             )
             goes, lacks = ((last_occ, first_occ), (first_occ, last_occ))[side]
-            pl.when(jnp.logical_not(goes))(move.start)
+            pl.when(jnp.logical_not(goes))(move(k, side).start)
             pl.when(lacks)(stand_in.start)
+
+    loan = pltpu.make_async_remote_copy(
+        src_ref=source_of(OWN_LOAN),
+        dst_ref=windows[BORROWED].at[pl.ds(orbs, orbs)],
+        send_sem=loan_sem.at[0],
+        recv_sem=loan_sem.at[1],
+        device_id=(occ_me, top - aux_me),
+        device_id_type=MESH,
+    )
+    for k in range(FINAL):
+        start_moves(k)
+    pl.when(late)(loan.start)
+    pl.when(jnp.logical_not(late))(lambda: start_moves(OWN_LOAN))
+    pl.when(jnp.logical_not(early))(lambda: start_moves(FINAL))
 
     @pl.when(aux_me > 0)
     def _():
@@ -124,11 +146,9 @@
         small.start()
         smalls.append(small)
     fetches = []
-    for k, (start, width) in enumerate(zip(starts, WIDTHS)):
+    for k in range(BORROWED):
         fetch = pltpu.make_async_copy(
-            ao.at[:, :, pl.ds(start, width)],
-            windows[k].at[pl.ds(orbs, orbs)],
-            local_sem.at[k],
+            source_of(k), windows[k].at[pl.ds(orbs, orbs)], local_sem.at[k]
         )
         fetch.start()
         fetches.append(fetch)
@@ -167,10 +187,10 @@
         row = jnp.broadcast_to(energies[pl.ds(s, 1), :], (pnos, pnos))
         scale[place] = -1.0 / (row + row.T - shift)
 
-    for k, (start, width) in enumerate(zip(starts, WIDTHS)):
-        fetches[k].wait()
-
-        def project(o, carry):
+    def project(k):
+        start, width = starts[k], WIDTHS[k]
+
+        def of_orbital(o, carry):
             block = windows[k][orbs + o]
             turned = coef_t[pl.ds(o * per_orbital, per_orbital)]
             own = jnp.dot(
@@ -180,7 +200,14 @@
             own_proj[pl.ds(o * per_orbital, per_orbital), :rows, start:start + width] = own
             return carry
 
-        lax.fori_loop(0, orbs, project, 0)
+        lax.fori_loop(0, orbs, of_orbital, 0)
+
+    for k in range(BORROWED):
+        fetches[k].wait()
+        if k == OWN_LOAN:
+            pl.when(jnp.logical_not(late))(lambda: project(OWN_LOAN))
+        else:
+            project(k)
 
     def pack(top, rest, strip_rows):
         corner = rest[:, LANES:]
@@ -212,11 +239,10 @@
         return [pack(*terms) for terms in zip(tops, rests, strips)]
 
     def arrive(k):
-        moves[2 * k].wait_recv()
-        moves[2 * k + 1].wait_recv()
-
-    last = len(WIDTHS) - 1
-    for k in range(last):
+        for side in range(2):
+            move(k, side).wait_recv()
+
+    def add_piece(k):
         arrive(k)
 
         def accumulate(number, carry):
@@ -226,6 +252,20 @@
             return carry
 
         lax.fori_loop(0, pairs // GROUP, accumulate, 0)
+
+    add_piece(0)
+    add_piece(1)
+
+    @pl.when(early)
+    def _():
+        loan.wait_recv()
+        start_moves(BORROWED)
+        start_moves(FINAL)
+        project(BORROWED)
+
+    add_piece(2)
+    pl.when(jnp.logical_not(late))(lambda: add_piece(OWN_LOAN))
+    pl.when(early)(lambda: add_piece(BORROWED))
 
     def pair_at(position):
         distance, place = ORDER[position]
@@ -266,10 +306,10 @@
     def _():
         pl.semaphore_wait(ready, 2)
 
-    arrive(last)
+    arrive(FINAL)
     for first in range(0, pairs, GROUP):
         group = [pair_at(position) for position in range(first, first + GROUP)]
-        totals = [sums[s] + part for s, part in zip(group, partials(group, last))]
+        totals = [sums[s] + part for s, part in zip(group, partials(group, FINAL))]
         for s, total in zip(group, totals):
             if first > 0:
                 sums[s] = total
@@ -380,15 +420,20 @@
     )
 
     for side, goes in enumerate((last_occ, first_occ)):
+        main = ao.at[:, :, pl.ds(0, starts[OWN_LOAN])]
         moved = pltpu.make_async_remote_copy(
-            src_ref=ao,
-            dst_ref=ao,
-            send_sem=ao_send.at[side],
+            src_ref=main,
+            dst_ref=main,
+            send_sem=ao_send.at[side, 0],
             recv_sem=ao_recv.at[side, 0],
             device_id=(right, aux_me),
             device_id_type=MESH,
         )
-        unless(goes, moved.wait_send)
+        stays = jnp.logical_not(goes)
+        pl.when(stays)(moved.wait_send)
+        pl.when(jnp.logical_and(stays, jnp.logical_not(late)))(move(OWN_LOAN, side).wait_send)
+        pl.when(jnp.logical_and(stays, early))(move(BORROWED, side).wait_send)
+    pl.when(late)(loan.wait_send)
     pltpu.make_async_remote_copy(
         src_ref=parcel,
         dst_ref=landed,
@@ -402,7 +447,7 @@
 
 
 def shards(mesh, ao_blocks, pno_coef, pno_energy, occ_energy, pair_partner, pno_count):
-    orbs, virtuals, aux_block = ao_blocks.shape
+    orbs, virtuals, _ = ao_blocks.shape
     pairs, _, pnos = pno_coef.shape
     occ_size, aux_size = mesh.shape["occ"], mesh.shape["aux"]
     rows = -(-pnos // 16) * 16
@@ -428,7 +473,7 @@
             pltpu.VMEM((pairs, pnos), F32),
             pltpu.VMEM((pairs, pnos, virtuals), BF16),
             pltpu.VMEM((pairs, rows, virtuals), BF16),
-            pltpu.VMEM((pairs, padded, aux_block), BF16),
+            pltpu.VMEM((pairs, padded, sum(WIDTHS)), BF16),
             pltpu.VMEM((pairs, packed, LANES), F32),
             pltpu.VMEM((MESSAGES, packed, LANES), BF16),
             pltpu.VMEM((MESSAGES, packed, LANES), BF16),
@@ -440,9 +485,10 @@
         + [pltpu.VMEM((3 * orbs, virtuals, width), BF16) for width in WIDTHS]
         + [
             dma((5,)),
-            dma((chunks,)),
+            dma((BORROWED,)),
+            dma((2, 3)),
+            dma((2, chunks)),
             dma((2,)),
-            dma((2, chunks)),
             dma,
             dma((MESSAGES, 2)),
             dma((3,)),

time: 59.7 us -> 59 us (0.988)
  Pallas kernels: 57.7 us -> 57 us
    pallas_call x1, Pallas kernels: 57.7 us -> 57 us  [shards(): pl.pallas_call(functools.partial(kernel, occ_size, aux_size), out_shape=(...]
where the time goes in v7:
time: 59 us; the launch traced here: 58.9 us
  Pallas kernels  57 us (97%)
  local copies, waits for them, and re-layouts  1.26 us (2%)
  between operations  0.64 us (1%)
    pallas_call x1, Pallas kernels, shards(): pl.pallas_call(functools.partial(kernel, occ_size, aux_size), out_shape=(...  57 us

profile of v7, /device:TPU:29, one launch (start us, length us, event | category | flops | bytes accessed | tf_op | source)
XLA Modules:
  0.0 58.9 jit_solution(15278194952229645463)
XLA Ops:
  0.6 57.0 %shard_map.77 = (f32[2,200,200]{2,1,0:T(8,128)S(1)}, f32[8,128]{1,0:T(8,128)S(1)}) custom-call(s32[16]{0:T(128)} %partner_in.1, s32[16]{0:T(128)} %counts_in.1, f32[256]{0:T(256)} %occ_energy_in.1, f32[16,200]{1,0:T(8,128)} %energies_in.1, bf16[4,256,1024]{2,1,0:T(8,128)(2,1)} %ao.1, bf16[16,200,256]{2,1,0:T(8,128)(2,1)} %bitcast.3), custom_call_target="tpu_custom_call" | custom-call | tf_op jit(solution)/shard_map/pallas_call | solution.py:461
  57.6 0.5 slice_bitcast_fusion
  58.2 0.8 %copy.9 = f32[2,200,200]{2,1,0:T(8,128)} copy(f32[2,200,200]{2,1,0:T(8,128)S(1)} %get-tuple-element.8) | data formatting | bytes 640000

commit v8 on v7

--- a/solution.py
+++ b/solution.py
@@ -127,7 +127,7 @@
         start_moves(k)
     pl.when(late)(loan.start)
     pl.when(jnp.logical_not(late))(lambda: start_moves(OWN_LOAN))
-    pl.when(jnp.logical_not(early))(lambda: start_moves(FINAL))
+    start_moves(FINAL)
 
     @pl.when(aux_me > 0)
     def _():
@@ -255,24 +255,21 @@
 
     add_piece(0)
     add_piece(1)
+    add_piece(2)
 
     @pl.when(early)
     def _():
         loan.wait_recv()
         start_moves(BORROWED)
-        start_moves(FINAL)
         project(BORROWED)
 
-    add_piece(2)
     pl.when(jnp.logical_not(late))(lambda: add_piece(OWN_LOAN))
-    pl.when(early)(lambda: add_piece(BORROWED))
+    pl.when(early)(lambda: add_piece(FINAL))
 
     def pair_at(position):
         distance, place = ORDER[position]
         return 2 * aux_at(distance) + place
 
-    messages = {}
-
     def number_of(chain, step):
         return sum(len(CHAINS[c][1]) for c in range(chain)) + step
 
@@ -280,10 +277,9 @@
     middle = -(-packed // 32) * 16
     halves = (pl.ds(0, middle), pl.ds(middle, packed - middle))
 
-    def send(chain, step, half, total):
+    def message(chain, step, half):
         number = number_of(chain, step)
-        parcel[number, halves[half]] = total.astype(BF16)
-        message = pltpu.make_async_remote_copy(
+        return pltpu.make_async_remote_copy(
             src_ref=parcel.at[number, halves[half]],
             dst_ref=landed.at[number, halves[half]],
             send_sem=chain_send,
@@ -291,11 +287,13 @@
             device_id=(occ_me, aux_at(CHAINS[chain][0])),
             device_id_type=MESH,
         )
-        message.start()
-        messages[chain, step, half] = message
+
+    def send(chain, step, half, total):
+        parcel[number_of(chain, step), halves[half]] = total.astype(BF16)
+        message(chain, step, half).start()
 
     def arrived(chain, step, half):
-        messages[chain, step, half].wait_recv()
+        message(chain, step, half).wait_recv()
         return landed[number_of(chain, step), halves[half]].astype(F32)
 
     @pl.when(jnp.logical_and(aux_me > 0, aux_me < top))
@@ -306,18 +304,21 @@
     def _():
         pl.semaphore_wait(ready, 2)
 
-    arrive(FINAL)
-    for first in range(0, pairs, GROUP):
-        group = [pair_at(position) for position in range(first, first + GROUP)]
-        totals = [sums[s] + part for s, part in zip(group, partials(group, FINAL))]
-        for s, total in zip(group, totals):
-            if first > 0:
-                sums[s] = total
-        if first == 0:
-            for chains in ((0, 1), (2, 3)):
+    def start_chains(k):
+        arrive(k)
+        for first, size_of in ((0, 2), (2, 2), *((i, GROUP) for i in range(GROUP, pairs, GROUP))):
+            group = [pair_at(position) for position in range(first, first + size_of)]
+            totals = [sums[s] + part for s, part in zip(group, partials(group, k))]
+            if first >= GROUP:
+                for s, total in zip(group, totals):
+                    sums[s] = total
+            else:
                 for half, part in enumerate((slice(0, middle), slice(middle, packed))):
-                    for chain in chains:
-                        send(chain, 0, half, totals[chain][part])
+                    for i in range(size_of):
+                        send(first + i, 0, half, totals[i][part])
+
+    pl.when(early)(lambda: start_chains(BORROWED))
+    pl.when(jnp.logical_not(early))(lambda: start_chains(FINAL))
 
     for step in range(1, 4):
         for chains in ((0, 1), (2, 3)):

time: 59 us -> 58.9 us (level)
  the two profiles are of different devices: /device:TPU:29 before, /device:TPU:25 now
where the time goes in v8:
time: 58.9 us; the launch traced here: 58.8 us
  Pallas kernels  56.9 us (97%)
  local copies, waits for them, and re-layouts  1.26 us (2%)
  between operations  0.64 us (1%)
    pallas_call x1, Pallas kernels, shards(): pl.pallas_call(functools.partial(kernel, occ_size, aux_size), out_shape=(...  56.9 us

profile of v8, /device:TPU:25, one launch (start us, length us, event | category | flops | bytes accessed | tf_op | source)
XLA Modules:
  0.0 58.8 jit_solution(4551341807114190325)
XLA Ops:
  0.6 56.9 %shard_map.77 = (f32[2,200,200]{2,1,0:T(8,128)S(1)}, f32[8,128]{1,0:T(8,128)S(1)}) custom-call(s32[16]{0:T(128)} %partner_in.1, s32[16]{0:T(128)} %counts_in.1, f32[256]{0:T(256)} %occ_energy_in.1, f32[16,200]{1,0:T(8,128)} %energies_in.1, bf16[4,256,1024]{2,1,0:T(8,128)(2,1)} %ao.1, bf16[16,200,256]{2,1,0:T(8,128)(2,1)} %bitcast.3), custom_call_target="tpu_custom_call" | custom-call | tf_op jit(solution)/shard_map/pallas_call | solution.py:462
  57.5 0.5 slice_bitcast_fusion
  58.0 0.8 %copy.9 = f32[2,200,200]{2,1,0:T(8,128)} copy(f32[2,200,200]{2,1,0:T(8,128)S(1)} %get-tuple-element.8) | data formatting | bytes 640000

commit v9 on v7

--- a/solution.py
+++ b/solution.py
@@ -101,7 +101,7 @@
             src_ref=source_of(k),
             dst_ref=windows[k].at[pl.ds(slot, orbs)],
             send_sem=ao_send.at[side, max(k, FINAL) - FINAL],
-            recv_sem=ao_recv.at[side, k],
+            recv_sem=ao_recv.at[k],
             device_id=(target, aux_me),
             device_id_type=MESH,
         )
@@ -109,7 +109,7 @@
     def start_moves(k):
         for side, slot in enumerate((0, 2 * orbs)):
             stand_in = pltpu.make_async_copy(
-                source_of(k), windows[k].at[pl.ds(slot, orbs)], ao_recv.at[side, k]
+                source_of(k), windows[k].at[pl.ds(slot, orbs)], ao_recv.at[k]
             )
             goes, lacks = ((last_occ, first_occ), (first_occ, last_occ))[side]
             pl.when(jnp.logical_not(goes))(move(k, side).start)
@@ -239,8 +239,15 @@
         return [pack(*terms) for terms in zip(tops, rests, strips)]
 
     def arrive(k):
-        for side in range(2):
-            move(k, side).wait_recv()
+        both = windows[k].at[pl.ds(0, 2 * orbs)]
+        pltpu.make_async_remote_copy(
+            src_ref=both,
+            dst_ref=both,
+            send_sem=ao_send.at[0, 0],
+            recv_sem=ao_recv.at[k],
+            device_id=(right, aux_me),
+            device_id_type=MESH,
+        ).wait_recv()
 
     def add_piece(k):
         arrive(k)
@@ -425,7 +432,7 @@
             src_ref=main,
             dst_ref=main,
             send_sem=ao_send.at[side, 0],
-            recv_sem=ao_recv.at[side, 0],
+            recv_sem=ao_recv.at[0],
             device_id=(right, aux_me),
             device_id_type=MESH,
         )
@@ -462,7 +469,7 @@
         functools.partial(kernel, occ_size, aux_size),
         out_shape=(
             jax.ShapeDtypeStruct((share, pnos, pnos), F32),
-            jax.ShapeDtypeStruct((8, LANES), F32),
+            jax.ShapeDtypeStruct((1, LANES), F32),
         ),
         in_specs=[anywhere] * 6,
         out_specs=(vmem, vmem),
@@ -479,15 +486,15 @@
             pltpu.VMEM((MESSAGES, packed, LANES), BF16),
             pltpu.VMEM((share, pnos, pnos), F32),
             pltpu.VMEM((share, pnos - LANES, pnos - LANES), F32),
-            pltpu.VMEM((8, LANES), F32),
-            pltpu.VMEM((3 * aux_size, 8, LANES), F32),
+            pltpu.VMEM((1, LANES), F32),
+            pltpu.VMEM((3 * aux_size, 1, LANES), F32),
         ]
         + [pltpu.VMEM((3 * orbs, virtuals, width), BF16) for width in WIDTHS]
         + [
             dma((5,)),
             dma((BORROWED,)),
             dma((2, 3)),
-            dma((2, chunks)),
+            dma((chunks,)),
             dma((2,)),
             dma,
             dma((MESSAGES, 2)),

time: 59 us -> 58.8 us (level)
  the two profiles are of different devices: /device:TPU:29 before, /device:TPU:31 now
where the time goes in v9:
time: 58.8 us; the launch traced here: 58.7 us
  Pallas kernels  56.8 us (97%)
  local copies, waits for them, and re-layouts  1.26 us (2%)
  between operations  0.64 us (1%)
    pallas_call x1, Pallas kernels, shards(): pl.pallas_call(functools.partial(kernel, occ_size, aux_size), out_shape=(...  56.8 us

profile of v9, /device:TPU:31, one launch (start us, length us, event | category | flops | bytes accessed | tf_op | source)
XLA Modules:
  0.0 58.7 jit_solution(11590896945548980592)
XLA Ops:
  0.6 56.8 %shard_map.77 = (f32[2,200,200]{2,1,0:T(8,128)S(1)}, f32[1,128]{1,0:T(1,128)S(1)}) custom-call(s32[16]{0:T(128)} %partner_in.1, s32[16]{0:T(128)} %counts_in.1, f32[256]{0:T(256)} %occ_energy_in.1, f32[16,200]{1,0:T(8,128)} %energies_in.1, bf16[4,256,1024]{2,1,0:T(8,128)(2,1)} %ao.1, bf16[16,200,256]{2,1,0:T(8,128)(2,1)} %bitcast.3), custom_call_target="tpu_custom_call" | custom-call | tf_op jit(solution)/shard_map/pallas_call | solution.py:468
  57.4 0.5 slice_bitcast_fusion
  57.9 0.8 %copy.9 = f32[2,200,200]{2,1,0:T(8,128)} copy(f32[2,200,200]{2,1,0:T(8,128)S(1)} %get-tuple-element.8) | data formatting | bytes 640000
